TPU v7x, 256 devices: a whole 4x4x8 slice. The times are simulated.
256 devices in a mesh: dp: 8 (over y, core), cent: 32 (over x, z).
Axes of the slice: x: 4, y: 4, z: 8, core: 2. Of those that a mesh axis runs over, the one named last changes fastest.
Arguments:
- passages: bfloat16 [32768, 768], P(('dp', 'cent')), may hold values from -10 to 10
- queries: bfloat16 [1024, 768], P(('dp', 'cent')), may hold values from -10 to 10
- init_centroids: float32 [8192, 768], P('cent'), may hold values from -12 to 12
- pattern: int32 [1024, 4], replicated, may hold values from 0 to 255, all different within a row
- positive_offset: int32 [1024], replicated, may hold values from 0 to 127
Outputs:
- centroids: float32 [8192, 768], P('cent')
- loss: float32 [1024], P(('dp', 'cent'))
Inputs may be any that keep to these rules, and one draw needn't show every extreme that they name: `pattern`: each row names 4 different blocks.
All inputs are finite; a program needn't handle non-finite values.
Results may differ from a plain program's by a relative error of at most 0.0055.
Values may be sent and summed in bfloat16 or wider, within the bound.
A program may use at most 64 MiB of HBM per device.

v0:
```python
import jax
import jax.numpy as jnp
from jax import lax
from jax.sharding import PartitionSpec as P

BLOCK = 128
ITERS = 2


sharpness = 0.05
sharpening_factor = 0.05
prior_weight = 1.0


def merged(value, axis, join):
    pieces = jax.tree.map(lambda part: lax.all_gather(part, axis), value)
    head = jax.tree.map(lambda part: part[0], pieces)
    tail = jax.tree.map(lambda part: part[1:], pieces)
    so_far, _ = lax.scan(lambda so_far, section: (join(so_far, section), None), head, tail)
    return so_far


def combine_query(first, second):
    upper = jnp.maximum(first[0], second[0])
    total = first[1] * jnp.exp(first[0] - upper) + second[1] * jnp.exp(second[0] - upper)
    return (upper, total, first[2] + second[2])


def on_device(passages, queries, init_centroids, pattern, positive_offset):
    gathered = lax.all_gather(passages, "cent", axis=0, tiled=True)
    cluster_means = init_centroids
    for step_index in range(ITERS):
        centers_half = cluster_means.astype(jnp.bfloat16)
        cluster_center_norms = jnp.sum(cluster_means * cluster_means, axis=1)
        unnormalized_log_odds = sharpness * (
            2.0 * jnp.dot(gathered, centers_half.T, preferred_element_type=jnp.float32)
            - cluster_center_norms[None, :]
        )
        row_max = lax.pmax(jnp.max(unnormalized_log_odds, axis=1), "cent")
        weights_exp = jnp.exp(unnormalized_log_odds - row_max[:, None])
        row_total = lax.psum(jnp.sum(weights_exp, axis=1), "cent")
        resp = weights_exp / row_total[:, None]
        numer = lax.dot_general(
            resp.astype(jnp.bfloat16),
            gathered,
            (((0,), (0,)), ((), ())),
            preferred_element_type=jnp.float32,
        )
        counts = jnp.sum(resp, axis=0)
        numer, counts = lax.psum((numer, counts), "dp")
        cluster_means = (numer + prior_weight * cluster_means) / (counts[:, None] + prior_weight)
    query_collection = lax.all_gather(queries, ("dp", "cent"), axis=0, tiled=True)
    local_rows = passages.shape[0]
    linear = lax.axis_index(("dp", "cent"))
    first_row = linear * local_rows
    local_blocks = first_row // BLOCK + jnp.arange(local_rows // BLOCK, dtype=jnp.int32)
    paired_entries = jnp.any(pattern[:, :, None] == local_blocks[None, None, :], axis=1)
    allowed = jnp.repeat(paired_entries, BLOCK, axis=1)
    affinity_matrix = (
        jnp.dot(query_collection, passages.T, preferred_element_type=jnp.float32)
        * sharpening_factor
    )
    target_col = pattern[:, 0] * BLOCK + positive_offset - first_row
    columns = jnp.arange(local_rows, dtype=jnp.int32)
    positive = jnp.sum(
        jnp.where(columns[None, :] == target_col[:, None], affinity_matrix, 0.0), axis=1
    )
    local_max = jnp.max(jnp.where(allowed, affinity_matrix, -1e30), axis=1)
    local_total = jnp.sum(
        jnp.where(allowed, jnp.exp(affinity_matrix - local_max[:, None]), 0.0), axis=1
    )
    query_max, query_total, positive_all = merged(
        (local_max, local_total, positive), ("dp", "cent"), combine_query
    )
    whole_loss = jnp.log(query_total) + query_max - positive_all
    own_count = queries.shape[0]
    own_loss = lax.dynamic_slice_in_dim(whole_loss, linear * own_count, own_count, 0)
    return (cluster_means, own_loss)


def solution(mesh):
    placed = (P(("dp", "cent"), None), P(("dp", "cent"), None), P("cent", None), P(), P())
    return jax.shard_map(
        on_device,
        mesh=mesh,
        in_specs=placed,
        out_specs=(P("cent", None), P(("dp", "cent"))),
        check_vma=False,
    )
```

profile of v0, /device:TPU:1, one launch (start us, length us, event | category | flops | bytes accessed | tf_op | source)
XLA Modules:
  0.0 1375.7 jit_solution(4740807136776224495)
XLA Ops:
  8.7 109.8 %all-gather.18.cloned.1.call-done = bf16[256,4,768]{2,1,0:T(4,128)(2,1)} async-done(((bf16[1,4,768]{2,1,0:T(4,128)(2,1)}), bf16[256,4,768]{2,1,0:T(4,128)(2,1)}) %all-gather.18.cloned.1.call-update) | async-done | bytes 1572880 | tf_op jit(solution)/shard_map/all_gather | solution.py:52
  118.5 2.7 reshape.42
  121.3 2.2 select_reduce_fusion.2
  124.3 1.4 select_reduce_fusion
  127.1 97.7 %all-gather.12.cloned.1.call-done = f32[262144]{0:T(1024)} async-done(((f32[1024]{0:T(1024)}), f32[262144]{0:T(1024)}) %all-gather.12.cloned.1.call-update) | async-done | bytes 1048592 | tf_op jit(solution)/shard_map/all_gather | solution.py:16
  224.8 1.3 slice.37
  226.2 103.3 %all-gather.14.cloned.1.call-done = f32[262144]{0:T(1024)} async-done(((f32[1024]{0:T(1024)}), f32[262144]{0:T(1024)}) %all-gather.14.cloned.1.call-update) | async-done | bytes 1048592 | tf_op jit(solution)/shard_map/all_gather | solution.py:16
  329.5 1.3 slice.38
  330.8 1.1 reshape.39
  332.0 102.2 %all-gather.16.cloned.1.call-done = f32[262144]{0:T(1024)} async-done(((f32[1024]{0:T(1024)}), f32[262144]{0:T(1024)}) %all-gather.16.cloned.1.call-update) | async-done | bytes 1048592 | tf_op jit(solution)/shard_map/all_gather | solution.py:16
  434.1 1.3 slice.39
  435.4 1.1 reshape.40
  436.6 218.6 %while.14 = (s32[]{:T(128)}, f32[1024]{0:T(1024)S(1)}, f32[1024]{0:T(1024)S(1)}, f32[1024]{0:T(1024)S(1)}, f32[255,1024]{1,0:T(8,128)S(1)}, /*index=5*/f32[255,1024]{1,0:T(8,128)}, f32[255,1024]{1,0:T(8,128)}, s32[]{:T(128)}) while((s32[]{:T(128)}, f32[1024]{0:T(1024)S(1)}, f32[1024]{0:T(1024)S(1)}, f32[1024]{0:T(1024)S(1)}, ...), condition=%wide.region_21.22_spmd, body=%wide.region_20.21_spmd.sunk | while | flops 7170 | bytes 61541 | solution.py:19
  446.9 0.8 constant_dynamic-slice_fusion.5
  447.7 0.8 constant_dynamic-slice_fusion.5
  452.0 0.8 constant_dynamic-slice_fusion.5
  453.7 0.8 constant_dynamic-slice_fusion.5
  457.2 0.8 constant_dynamic-slice_fusion.5
  458.0 0.8 constant_dynamic-slice_fusion.5
  460.6 0.8 constant_dynamic-slice_fusion.5
  463.2 0.8 constant_dynamic-slice_fusion.5
  464.9 0.8 constant_dynamic-slice_fusion.5
  465.7 0.8 constant_dynamic-slice_fusion.5
  485.4 0.8 constant_dynamic-slice_fusion.5
  490.6 0.8 constant_dynamic-slice_fusion.5
  491.4 0.8 constant_dynamic-slice_fusion.5
  493.2 0.8 constant_dynamic-slice_fusion.5
  494.0 0.8 constant_dynamic-slice_fusion.5
  495.7 0.8 constant_dynamic-slice_fusion.5
  497.5 0.8 constant_dynamic-slice_fusion.5
  498.3 0.8 constant_dynamic-slice_fusion.5
  500.9 0.8 constant_dynamic-slice_fusion.5
  502.6 0.8 constant_dynamic-slice_fusion.5
  503.5 0.8 constant_dynamic-slice_fusion.5
  504.3 0.8 constant_dynamic-slice_fusion.5
  505.2 0.8 constant_dynamic-slice_fusion.5
  506.1 0.8 constant_dynamic-slice_fusion.5
  507.8 0.8 constant_dynamic-slice_fusion.5
  508.6 0.8 constant_dynamic-slice_fusion.5
  509.5 0.8 constant_dynamic-slice_fusion.5
  512.9 0.8 constant_dynamic-slice_fusion.5
  513.8 0.8 constant_dynamic-slice_fusion.5
  514.6 0.8 constant_dynamic-slice_fusion.5
  515.5 0.8 constant_dynamic-slice_fusion.5
  518.1 0.8 constant_dynamic-slice_fusion.5
  518.9 0.8 constant_dynamic-slice_fusion.5
  655.8 6.7 fusion.18
  662.4 114.8 %pmax.14 = f32[4096]{0:T(1024)S(1)} all-reduce(f32[4096]{0:T(1024)S(1)} %get-tuple-element.66), channel_id=1, replica_groups=mesh['dp'=8,'cent'=32] {'cent'}, use_global_device_ids=true, to_apply=%region_2.0 | all-reduce | flops 4096 | bytes 32768 | tf_op jit(solution)/shard_map/pmax | solution.py:39
  777.3 2.8 fusion.5
  780.1 110.4 %psum.42 = f32[4096]{0:T(1024)S(1)} all-reduce(f32[4096]{0:T(1024)S(1)} %fusion.5), channel_id=1, replica_groups=mesh['dp'=8,'cent'=32] {'cent'}, use_global_device_ids=true, to_apply=%region_4.0 | all-reduce | flops 4096 | bytes 32768 | tf_op jit(solution)/shard_map/psum | solution.py:41
  890.5 6.8 fusion.10
  897.4 3.0 fusion.14
  900.4 66.7 %psum.44 = f32[256]{0:T(256)S(1)} all-reduce(f32[256]{0:T(256)S(1)} %fusion.14), channel_id=1, replica_groups=mesh['dp'=8,'cent'=32] {'dp'}, use_global_device_ids=true, to_apply=%region_7.0 | all-reduce | flops 256 | bytes 2048 | tf_op jit(solution)/shard_map/psum | solution.py:50
  967.1 43.0 %all-reduce.3.cloned.1.call-done = f32[256,768]{1,0:T(8,128)} async-done(((f32[256,768]{1,0:T(8,128)}), f32[256,768]{1,0:T(8,128)}) %all-reduce.3.cloned.1.call-update) | async-done | bytes 786448 | tf_op jit(solution)/shard_map/psum | solution.py:50
  1010.1 1.4 multiply_reduce_fusion
  1011.5 6.7 fusion.19
  1018.1 115.5 %pmax.15 = f32[4096]{0:T(1024)S(1)} all-reduce(f32[4096]{0:T(1024)S(1)} %get-tuple-element.68), channel_id=1, replica_groups=mesh['dp'=8,'cent'=32] {'cent'}, use_global_device_ids=true, to_apply=%region_10.0 | all-reduce | flops 4096 | bytes 32768 | tf_op jit(solution)/shard_map/pmax | solution.py:39
  1133.6 2.8 fusion.6
  1136.4 110.9 %psum.45 = f32[4096]{0:T(1024)S(1)} all-reduce(f32[4096]{0:T(1024)S(1)} %fusion.6), channel_id=1, replica_groups=mesh['dp'=8,'cent'=32] {'cent'}, use_global_device_ids=true, to_apply=%region_12.0 | all-reduce | flops 4096 | bytes 32768 | tf_op jit(solution)/shard_map/psum | solution.py:41
  1247.3 6.8 fusion.8
  1254.1 3.0 fusion.12
  1257.1 69.0 %psum.47 = f32[256]{0:T(256)S(1)} all-reduce(f32[256]{0:T(256)S(1)} %fusion.12), channel_id=1, replica_groups=mesh['dp'=8,'cent'=32] {'dp'}, use_global_device_ids=true, to_apply=%region_15.0 | all-reduce | flops 256 | bytes 2048 | tf_op jit(solution)/shard_map/psum | solution.py:50
  1326.2 40.6 %all-reduce.5.cloned.1.call-done = f32[256,768]{1,0:T(8,128)} async-done(((f32[256,768]{1,0:T(8,128)}), f32[256,768]{1,0:T(8,128)}) %all-reduce.5.cloned.1.call-update) | async-done | bytes 786448 | tf_op jit(solution)/shard_map/psum | solution.py:50
  1366.7 2.1 add_divide_fusion
  (1021 shorter events, 187.0 us)
Async XLA Ops:
  7.2 117.1 %copy-start.1 = (s32[1024]{0:T(1024)S(1)}, s32[1024]{0:T(1024)}, u32[]{:S(2)}) copy-start(s32[1024]{0:T(1024)} %param.11) | copy-start | bytes 12292
  7.2 119.8 %copy-start = (f32[256,768]{1,0:T(8,128)S(1)}, f32[256,768]{1,0:T(8,128)}, u32[]{:S(2)}) copy-start(f32[256,768]{1,0:T(8,128)} %param.9) | copy-start | bytes 2359300
  7.2 111.3 %all-gather.18.cloned.1.call-start = ((), (), s32[]{:S(2)}) async-start(), calls=%async_computation.6 | async-start | bytes 1579008 | tf_op jit(solution)/shard_map/all_gather | solution.py:52
  7.9 216.8 %all-gather.12.cloned.1.call-start = ((), (), s32[]{:S(2)}) async-start(), calls=%async_computation.3 | async-start | bytes 1052672 | tf_op jit(solution)/shard_map/all_gather | solution.py:16
  123.5 206.1 %all-gather.14.cloned.1.call-start = ((), (), s32[]{:S(2)}) async-start(), calls=%async_computation.4 | async-start | bytes 1052672 | tf_op jit(solution)/shard_map/all_gather | solution.py:16
  125.7 308.4 %all-gather.16.cloned.1.call-start = ((), (), s32[]{:S(2)}) async-start(), calls=%async_computation.5 | async-start | bytes 1052672 | tf_op jit(solution)/shard_map/all_gather | solution.py:16
  126.3 529.5 %all-gather.10.cloned.1.call-start = ((), (), s32[]{:S(2)}) async-start(), calls=%async_computation | async-start | bytes 6488064 | tf_op jit(solution)/shard_map/all_gather | solution.py:30
  126.9 883.2 %all-reduce.3.cloned.1.call-start = ((), (), s32[]{:S(2)}) async-start(), calls=%async_computation.1 | async-start | bytes 1572864 | tf_op jit(solution)/shard_map/psum | solution.py:50
  226.2 210.3 %slice-start = ((f32[262144]{0:T(1024)}), f32[1024]{0:T(1024)S(1)}, s32[]{:S(2)}) async-start(f32[262144]{0:T(1024)} %all-gather.12.cloned.1.call-done), calls=%async_computation.7 | async-start | bytes 8192 | tf_op jit(solution)/shard_map/slice | solution.py:17
  329.5 107.0 %slice-start.1 = ((f32[262144]{0:T(1024)}), f32[1024]{0:T(1024)S(1)}, s32[]{:S(2)}) async-start(f32[262144]{0:T(1024)} %all-gather.14.cloned.1.call-done), calls=%async_computation.8 | async-start | bytes 8192 | tf_op jit(solution)/shard_map/slice | solution.py:17
  434.1 2.4 slice-start.2
  897.3 469.4 %all-reduce.5.cloned.1.call-start = ((), (), s32[]{:S(2)}) async-start(), calls=%async_computation.2 | async-start | bytes 1572864 | tf_op jit(solution)/shard_map/psum | solution.py:50
Sparse Core Ops, SparseCore 0:
  11.6 106.9 all-gather.17
  123.6 101.1 all-gather.11
  228.5 100.9 all-gather.13
  333.1 100.9 all-gather.15
  436.6 86.8 all-gather.9
  897.5 112.5 all-reduce.2
  1254.2 112.4 all-reduce.4
where the time goes:
time: 1400 us; the launch traced here: 1380 us
  blocking collectives  587 us (42%)
  waiting for transfers between devices  498 us (36%)
  local copies, waits for them, and re-layouts  214 us (15%)
  matrix products  29.1 us (2%)
  other arithmetic  22.3 us (2%)
  between operations  14.2 us (1%)
    all_gather x3, waiting for transfers between devices, merged(): pieces = jax.tree.map(lambda part: lax.all_gather(part, axis), value)  303 us
    pmax x2, blocking collectives, on_device(): row_max = lax.pmax(jnp.max(unnormalized_log_odds, axis=1), 'cent')  230 us
    psum x2, blocking collectives, on_device(): row_total = lax.psum(jnp.sum(weights_exp, axis=1), 'cent')  221 us
    dynamic_slice x510, local copies, waits for them, and re-layouts, merged(): lax.scan(lambda so_far, section: (join(so_far, section), None), head, tail)  204 us
    psum x2, blocking collectives, on_device(): numer, counts = lax.psum((numer, counts), 'dp')  136 us
    all_gather x1, waiting for transfers between devices, on_device(): lax.all_gather(queries, ('dp', 'cent'), axis=0, tiled=True)  110 us
    psum x2, waiting for transfers between devices, on_device(): numer, counts = lax.psum((numer, counts), 'dp')  83.6 us
  transfers between devices with their start and end apart: 7, of which 6 were waited for; matrix products, arithmetic and copies ran while one was open for 16% of the time, Pallas kernels for 0%

commit v1 on v0

v1 whole, which is shorter than its diff:
```python
import jax
import jax.numpy as jnp
from jax import lax
from jax.experimental import pallas as pl
from jax.experimental.pallas import tpu as pltpu
from jax.sharding import PartitionSpec as P

MESH = pl.DeviceIdType.MESH
BLOCK = 128
D = 768
NX, NZ, NY = 4, 8, 4
CENT = NX * NZ
DP = 2 * NY
KL = 256
QP = 64
W = D + 128
sharpness = 0.05
NEG = -1e30
F32 = jnp.float32
BF16 = jnp.bfloat16


def rcopy(src, dst, ss, rs, dev):
    return pltpu.make_async_remote_copy(
        src_ref=src, dst_ref=dst, send_sem=ss, recv_sem=rs, device_id=dev, device_id_type=MESH
    )


def kernel(
    p_ref, q_ref, c_ref, meta_ref, out_ref, loss_ref,
    G, E, S, CQ, C2, NB, acc, rb1, rb2, own, st_s, st_r, rs_r,
    qs, qr, qp_s, qp_r,
    g_ss, g_rs, q_ss, q_rs, st_ss, st_rs, rs_ss, rs_rs,
    n1_s, n2_ss, n2_rs, c_ss, c_rs, f_ss, f_rs, qp_ss, qp_rs, loc,
):
    dp = lax.axis_index("dp")
    me = lax.axis_index("cent")
    x, z = me // NZ, me % NZ
    y, core = dp // 2, dp % 2
    sib = (dp + 1 - 2 * core, me)

    def cdev(xx, zz):
        return (dp, xx * NZ + zz)

    barrier = pltpu.get_barrier_semaphore()

    def sig_cent(o, _):
        pl.semaphore_signal(barrier, inc=1, device_id=(dp, (me + o) % CENT), device_id_type=MESH)
        return 0

    lax.fori_loop(1, CENT, sig_cent, 0)

    def sig_dp(o, _):
        pl.semaphore_signal(barrier, inc=1, device_id=((dp + o) % DP, me), device_id_type=MESH)
        return 0

    lax.fori_loop(1, DP, sig_dp, 0)
    own_copy = pltpu.make_async_copy(p_ref, G.at[z, x], loc)
    own_copy.start()
    qs[...] = jnp.zeros_like(qs)
    qs[0:4, :] = q_ref[...].astype(F32)
    qr[dp] = qs[...]
    c0 = c_ref[...]
    CQ[0:KL, :] = c0.astype(BF16)
    NB[0] = jnp.broadcast_to(jnp.sum(c0 * c0, axis=1, keepdims=True), (KL, 128))
    pl.semaphore_wait(barrier, CENT + DP - 2)

    def q_copy(o, src):
        return rcopy(qs, qr.at[src], q_ss.at[o], q_rs.at[src], ((dp + o) % DP, me))

    def q_send(o, _):
        q_copy(o, dp).start()
        return 0

    lax.fori_loop(1, DP, q_send, 0)

    def g_copy(o, xs, zs):
        peer = (me + o) % CENT
        return rcopy(p_ref, G.at[zs, xs], g_ss.at[o], g_rs.at[zs, xs], (dp, peer))

    def g_send(o, _):
        g_copy(o, x, z).start()
        return 0

    lax.fori_loop(1, CENT, g_send, 0)

    def q_wait(o, _):
        q_copy(o, (dp + DP - o) % DP).wait_recv()
        return 0

    lax.fori_loop(1, DP, q_wait, 0)
    CQ[KL:KL + QP, :] = qr[...].reshape(QP, D).astype(BF16)
    own_copy.wait()

    def column(k):
        d = (k + 1) // 2
        sgn = 1 - 2 * (k % 2)
        return (z + NZ + sgn * d) % NZ

    def g_wait(zc, xc):
        g_copy(1, xc, zc).wait_recv()

    def st_copy(it, xc, zc, xs, zs):
        return rcopy(
            st_s.at[zc, xc], st_r.at[it, zs, xs], st_ss.at[zc, xc], st_rs.at[it, zs, xs], cdev(xc, zc)
        )

    def logits(it, zc, lhs):
        pc = G[zc].reshape(NX * BLOCK, D)
        dots = lax.dot_general(lhs, pc, (((1,), (1,)), ((), ())), preferred_element_type=F32)
        nb = NB[it]
        for xc in range(NX):
            lo = xc * BLOCK
            ll = sharpness * (2.0 * dots[0:KL, lo:lo + BLOCK] - nb)
            m = jnp.max(ll, axis=0, keepdims=True)
            e = jnp.exp(ll - m)
            s = jnp.sum(e, axis=0, keepdims=True)
            E[zc, :, lo:lo + BLOCK] = e
            st_s[zc, xc, 0:1, :] = m
            st_s[zc, xc, 1:2, :] = s
        if it == 0:
            S[zc] = dots[KL:KL + QP, :] * sharpness

    def softmax_pass(it, lhs_of):
        if it == 0:
            for i in range(1, NX):
                g_wait(z, (x + i) % NX)
        logits(it, z, lhs_of())
        st_r[it, z, x] = st_s[z, x]
        for i in range(1, NX):
            st_copy(it, (x + i) % NX, z, x, z).start()

        def col_step(k, _):
            zc = column(k)
            if it == 0:
                for xc in range(NX):
                    g_wait(zc, xc)
            logits(it, zc, lhs_of())
            for xc in range(NX):
                st_copy(it, xc, zc, x, z).start()
            return 0

        lax.fori_loop(1, NZ, col_step, 0)

    def rs_copy(it, o, xo, zo):
        peer = (me + o) % CENT
        return rcopy(
            rs_r.at[it, z, x], rs_r.at[it, zo, xo], rs_ss.at[it, o], rs_rs.at[it, zo, xo], (dp, peer)
        )

    def owner_combine(it):
        def w(o, _):
            src = (me + o) % CENT
            st_copy(it, x, z, src // NZ, src % NZ).wait_recv()
            return 0

        lax.fori_loop(1, CENT, w, 0)
        m = st_r[it, :, :, 0:1, :].reshape(CENT, 1, BLOCK)
        s = st_r[it, :, :, 1:2, :].reshape(CENT, 1, BLOCK)
        top = jnp.max(m, axis=0)
        tot = jnp.sum(s * jnp.exp(m - top[None]), axis=0)
        rs_r[it, z, x, 0:1, :] = top
        rs_r[it, z, x, 1:2, :] = 1.0 / tot

        def snd(o, _):
            rs_copy(it, o, x, z).start()
            return 0

        lax.fori_loop(1, CENT, snd, 0)

    def query_post():
        meta = meta_ref[...]
        pats = [jnp.broadcast_to(meta[:, i:i + 1], (QP, BLOCK)) for i in range(4)]
        off = jnp.broadcast_to(meta[:, 4:5], (QP, BLOCK))
        lane = lax.broadcasted_iota(jnp.int32, (QP, BLOCK), 1)

        def allow_of(b):
            return (pats[0] == b) | (pats[1] == b) | (pats[2] == b) | (pats[3] == b)

        def p1(zc, mx):
            for xc in range(NX):
                b = dp * CENT + xc * NZ + zc
                sv = S[zc, :, xc * BLOCK:(xc + 1) * BLOCK]
                mx = jnp.maximum(mx, jnp.where(allow_of(b), sv, NEG))
            return mx

        mx = lax.fori_loop(0, NZ, p1, jnp.full((QP, BLOCK), NEG, F32))
        mrow = jnp.max(mx, axis=1, keepdims=True)
        mb = jnp.broadcast_to(mrow, (QP, BLOCK))

        def p2(zc, carry):
            tot, pos = carry
            for xc in range(NX):
                b = dp * CENT + xc * NZ + zc
                sv = S[zc, :, xc * BLOCK:(xc + 1) * BLOCK]
                tot = tot + jnp.where(allow_of(b), jnp.exp(sv - mb), 0.0)
                pos = pos + jnp.where((pats[0] == b) & (lane == off), sv, 0.0)
            return tot, pos

        zero = jnp.zeros((QP, BLOCK), F32)
        tot, pos = lax.fori_loop(0, NZ, p2, (zero, zero))
        trow = jnp.broadcast_to(jnp.sum(tot, axis=1, keepdims=True), (QP, BLOCK))
        prow = jnp.broadcast_to(jnp.sum(pos, axis=1, keepdims=True), (QP, BLOCK))
        packed = jnp.where(lane == 0, mb, jnp.where(lane == 1, trow, prow))
        qp_s[...] = packed.reshape(DP, 8, BLOCK)
        qp_r[dp] = qp_s[dp]

        def snd(o, _):
            qp_copy(o, (dp + o) % DP, dp).start()
            return 0

        lax.fori_loop(1, DP, snd, 0)

    def qp_copy(o, dst, src):
        return rcopy(qp_s.at[dst], qp_r.at[src], qp_ss.at[o], qp_rs.at[src], (dst, me))

    def query_finish():
        def w(o, _):
            qp_copy(o, (dp + o) % DP, (dp + o) % DP).wait_recv()
            return 0

        lax.fori_loop(1, DP, w, 0)
        m = qp_r[:, :, 0:1]
        t = qp_r[:, :, 1:2]
        p = qp_r[:, :, 2:3]
        top = jnp.max(m, axis=0)
        tot = jnp.sum(t * jnp.exp(m - top[None]), axis=0)
        ps = jnp.sum(p, axis=0)
        loss_ref[...] = jnp.broadcast_to(jnp.log(tot) + top - ps, (8, BLOCK))

        def ws(o, _):
            qp_copy(o, (dp + o) % DP, dp).wait_send()
            return 0

        lax.fori_loop(1, DP, ws, 0)

    def numer_pass(it):
        def w(o, _):
            src = (me + o) % CENT
            rs_copy(it, o, src // NZ, src % NZ).wait_recv()
            return 0

        lax.fori_loop(1, CENT, w, 0)
        acc[...] = jnp.zeros_like(acc)

        def col(zc, _):
            cnt = acc[:, D:W]
            parts = []
            for xc in range(NX):
                g = jnp.exp(st_s[zc, xc, 0:1, :] - rs_r[it, zc, xc, 0:1, :]) * rs_r[it, zc, xc, 1:2, :]
                r = E[zc, :, xc * BLOCK:(xc + 1) * BLOCK] * g
                cnt = cnt + r
                parts.append(r.astype(BF16))
            acc[:, D:W] = cnt
            r_all = jnp.concatenate(parts, axis=1)
            acc[:, 0:D] += jnp.dot(r_all, G[zc].reshape(NX * BLOCK, D), preferred_element_type=F32)
            return 0

        lax.fori_loop(0, NZ, col, 0)

        def ws(o, _):
            dst = (me + o) % CENT
            st_copy(it, dst // NZ, dst % NZ, x, z).wait_send()
            rs_copy(it, o, x, z).wait_send()
            return 0

        lax.fori_loop(1, CENT, ws, 0)

    half = pl.multiple_of(core * 128, 128)
    other = pl.multiple_of(128 - core * 128, 128)
    myrow = pl.multiple_of(core * 128 + y * 32, 32)

    def reduce_dp(it):
        c1 = rcopy(acc.at[pl.ds(other, 128)], rb1.at[it], n1_s.at[it, 0], n1_s.at[it, 1], sib)
        c1.start()
        c1.wait_recv()
        acc[pl.ds(half, 128), :] += rb1[it]
        cs = []
        for i in range(1, NY):
            yp = (y + i) % NY
            rows = pl.ds(pl.multiple_of(core * 128 + yp * 32, 32), 32)
            c = rcopy(acc.at[rows], rb2.at[it, i - 1], n2_ss.at[it, i - 1], n2_rs.at[it, i - 1], (yp * 2 + core, me))
            c.start()
            cs.append(c)
        tot = acc[pl.ds(myrow, 32), :]
        for i in range(NY - 1):
            cs[i].wait_recv()
            tot = tot + rb2[it, i]
        c1.wait_send()
        for c in cs:
            c.wait_send()
        counts = jnp.sum(tot[:, D:W], axis=1, keepdims=True)
        cold = c_ref[pl.ds(myrow, 32), :] if it == 0 else own[...]
        return (tot[:, 0:D] + cold) / (counts + 1.0)

    def spread(arr, ss, rs, k):
        rows = arr.at[pl.ds(myrow, 32)]
        cs = []
        for i in range(1, NY):
            yp = (y + i) % NY
            cs.append(rcopy(rows, rows, ss.at[k, i - 1], rs.at[k, i - 1], (yp * 2 + core, me)))
        cs.append(rcopy(rows, rows, ss.at[k, 3], rs.at[k, 3], sib))
        return cs

    def all_gather_rows(arrs, ss, rs):
        groups = [spread(a, ss, rs, k) for k, a in enumerate(arrs)]
        for i in range(NY):
            for g in groups:
                g[i].start()
        fw = []
        for i in range(1, NY):
            ysrc = (y + NY - i) % NY
            rows = pl.ds(pl.multiple_of(core * 128 + ysrc * 32, 32), 32)
            for k, a in enumerate(arrs):
                groups[k][i - 1].wait_recv()
                c = rcopy(a.at[rows], a.at[rows], ss.at[k, 3 + i], rs.at[k, 3 + i], sib)
                c.start()
                fw.append(c)
        for g in groups:
            g[3].wait_recv()
        for c in fw:
            c.wait_recv()
        for g in groups:
            for c in g:
                c.wait_send()
        for c in fw:
            c.wait_send()

    softmax_pass(0, lambda: CQ[...])
    owner_combine(0)
    query_post()
    numer_pass(0)
    newc = reduce_dp(0)
    own[...] = newc
    C2[pl.ds(myrow, 32), :] = newc.astype(BF16)
    NB[1, pl.ds(myrow, 32), :] = jnp.broadcast_to(jnp.sum(newc * newc, axis=1, keepdims=True), (32, 128))
    all_gather_rows([C2, NB.at[1]], c_ss, c_rs)

    softmax_pass(1, lambda: C2[...])
    owner_combine(1)
    query_finish()
    numer_pass(1)
    out_ref[pl.ds(myrow, 32), :] = reduce_dp(1)
    all_gather_rows([out_ref], f_ss, f_rs)

    def ws(o, _):
        g_copy(o, x, z).wait_send()
        return 0

    lax.fori_loop(1, CENT, ws, 0)

    def wsq(o, _):
        q_copy(o, dp).wait_send()
        return 0

    lax.fori_loop(1, DP, wsq, 0)


def on_device(passages, queries, init_centroids, pattern, positive_offset):
    me = lax.axis_index("cent")
    meta = jnp.concatenate([pattern, positive_offset[:, None]], axis=1).reshape(DP, CENT, 4, 5)
    meta = lax.dynamic_index_in_dim(meta, me, 1, keepdims=False)
    meta = jnp.pad(meta, ((0, 0), (0, 4), (0, 123)), constant_values=-1).reshape(QP, 128)
    vm = pl.BlockSpec(memory_space=pltpu.VMEM)
    dma = pltpu.SemaphoreType.DMA
    centroids, loss = pl.pallas_call(
        kernel,
        out_shape=(jax.ShapeDtypeStruct((KL, D), F32), jax.ShapeDtypeStruct((8, 128), F32)),
        in_specs=[vm] * 4,
        out_specs=(vm, vm),
        scratch_shapes=[
            pltpu.VMEM((NZ, NX, BLOCK, D), BF16),
            pltpu.VMEM((NZ, KL, NX * BLOCK), F32),
            pltpu.VMEM((NZ, QP, NX * BLOCK), F32),
            pltpu.VMEM((KL + QP, D), BF16),
            pltpu.VMEM((KL, D), BF16),
            pltpu.VMEM((2, KL, 128), F32),
            pltpu.VMEM((KL, W), F32),
            pltpu.VMEM((2, 128, W), F32),
            pltpu.VMEM((2, NY - 1, 32, W), F32),
            pltpu.VMEM((32, D), F32),
            pltpu.VMEM((NZ, NX, 2, 128), F32),
            pltpu.VMEM((2, NZ, NX, 2, 128), F32),
            pltpu.VMEM((2, NZ, NX, 2, 128), F32),
            pltpu.VMEM((8, D), F32),
            pltpu.VMEM((DP, 8, D), F32),
            pltpu.VMEM((DP, 8, 128), F32),
            pltpu.VMEM((DP, 8, 128), F32),
            dma((CENT,)), dma((NZ, NX)),
            dma((DP,)), dma((DP,)),
            dma((NZ, NX)), dma((2, NZ, NX)),
            dma((2, CENT)), dma((2, NZ, NX)),
            dma((2, 2)), dma((2, 3)), dma((2, 3)),
            dma((2, 8)), dma((2, 8)),
            dma((1, 8)), dma((1, 8)),
            dma((DP,)), dma((DP,)),
            dma,
        ],
        compiler_params=pltpu.CompilerParams(
            collective_id=0, has_side_effects=True, vmem_limit_bytes=40 * 1024 * 1024
        ),
    )(passages, queries, init_centroids, meta)
    return centroids, loss[:4, 0]


def solution(mesh):
    placed = (P(("dp", "cent"), None), P(("dp", "cent"), None), P("cent", None), P(), P())
    return jax.shard_map(
        on_device,
        mesh=mesh,
        in_specs=placed,
        out_specs=(P("cent", None), P(("dp", "cent"))),
        check_vma=False,
    )
```

time: 1400 us -> 250 us (0.18); the launches traced: 1380 us -> 250 us
  blocking collectives: 587 us -> 0 us
  waiting for transfers between devices: 498 us -> 0 us
  Pallas kernels: 0 us -> 244 us
  local copies, waits for them, and re-layouts: 214 us -> 4.73 us
  matrix products: 29.1 us -> 0 us
  other arithmetic: 22.3 us -> 0.09 us
    all_gather x5 -> x0, waiting for transfers between devices: 413 us -> none  [the longest x3 303 us: merged(): pieces = jax.tree.map(lambda part: lax.all_gather(part, axis), value)]
    psum x4 -> x0, blocking collectives: 357 us -> none  [the longest x2 221 us: on_device(): row_total = lax.psum(jnp.sum(weights_exp, axis=1), 'cent')]
    pallas_call x0 -> x1, Pallas kernels: none -> 244 us  [on_device(): pl.pallas_call(kernel, out_shape=(jax.ShapeDtypeStruct((KL, D), F32), jax...]
    pmax x2 -> x0, blocking collectives: 230 us -> none  [on_device(): row_max = lax.pmax(jnp.max(unnormalized_log_odds, axis=1), 'cent')]
    dynamic_slice x511 -> x0, local copies, waits for them, and re-layouts: 205 us -> none  [the longest x510 204 us: merged(): lax.scan(lambda so_far, section: (join(so_far, section), None), head, tail)]
    psum x2 -> x0, waiting for transfers between devices: 83.6 us -> none  [on_device(): numer, counts = lax.psum((numer, counts), 'dp')]
    dot_general x5 -> x0, matrix products: 29.1 us -> none  [the longest x2 13.6 us: on_device(): lax.dot_general(resp.astype(jnp.bfloat16), gathered, (((0,), (0,)), ((),...]
    reduce_sum x7 -> x0, other arithmetic: 14.5 us -> none  [the longest x2 5.96 us: on_device(): counts = jnp.sum(resp, axis=0)]
  transfers between devices with their start and end apart: 7 -> 0, of which waited for: 6 -> 0; matrix products, arithmetic and copies ran while one was open for 16% -> 0% of each run, Pallas kernels for 0% -> 0%
where the time goes in v1:
time: 250 us
  Pallas kernels  244 us (98%)
  local copies, waits for them, and re-layouts  4.73 us (2%)
    pallas_call x1, Pallas kernels, on_device(): pl.pallas_call(kernel, out_shape=(jax.ShapeDtypeStruct((KL, D), F32), jax...  244 us

profile of v1, /device:TPU:1, one launch (start us, length us, event | category | flops | bytes accessed | tf_op | source)
XLA Modules:
  0.0 250.0 jit_solution(15820430132306695847)
XLA Ops:
  0.6 0.0 copy-start.4
  0.6 0.7 copy-done.4
  1.3 0.0 copy-start.3
  1.3 0.1 concatenate.9
  1.5 0.0 copy-start
  1.5 0.1 copy.11
  1.6 0.5 copy-done.3
  2.0 0.5 concatenate.8
  2.6 0.3 copy.10
  2.9 0.0 copy-start.1
  2.9 0.1 dynamic-slice_add_fusion
  3.0 0.3 copy.15
  3.3 0.0 copy-start.2
  3.3 0.0 copy-done
  3.3 0.5 copy-done.1
  3.8 0.2 copy-done.2
  4.0 244.5 %shard_map.68 = (f32[256,768]{1,0:T(8,128)S(1)}, f32[8,128]{1,0:T(8,128)S(1)}) custom-call(bf16[128,768]{1,0:T(8,128)(2,1)S(1)} %copy-done.1, bf16[4,768]{1,0:T(4,128)(2,1)S(1)} %copy-done.2, f32[256,768]{1,0:T(8,128)S(1)} %copy-done, s32[64,128]{1,0:T(8,128)S(1)} %pad_bitcast_fusion.meta_ref), custom_call_target="tpu_custom_call" | custom-call | tf_op jit(solution)/shard_map/pallas_call | solution.py:366
  248.5 0.6 slice_reduce_fusion
  249.1 0.9 copy.17
  (1 shorter events, 0.0 us)
Async XLA Ops:
  0.6 0.7 copy-start.4
  1.3 0.7 copy-start.3
  1.5 1.8 copy-start
  2.9 0.9 copy-start.1
  3.3 0.7 copy-start.2

commit v2 on v1

--- a/solution.py
+++ b/solution.py
@@ -16,6 +16,9 @@
 W = D + 128
 sharpness = 0.05
 NEG = -1e30
+RA, RB = 80, 48
+HD = D // 2
+STOP = 99
 F32 = jnp.float32
 BF16 = jnp.bfloat16
 
@@ -30,8 +33,8 @@
     p_ref, q_ref, c_ref, meta_ref, out_ref, loss_ref,
     G, E, S, CQ, C2, NB, acc, rb1, rb2, own, st_s, st_r, rs_r,
     qs, qr, qp_s, qp_r,
-    g_ss, g_rs, q_ss, q_rs, st_ss, st_rs, rs_ss, rs_rs,
-    n1_s, n2_ss, n2_rs, c_ss, c_rs, f_ss, f_rs, qp_ss, qp_rs, loc,
+    az_ss, az_rs, bz_ss, bz_rs, ax_ss, ax_rs, bx_ss, bx_rs, q_ss, q_rs, st_ss, st_rs, rs_ss, rs_rs,
+    n1_s, n2_ss, n2_rs, c_ss, c_rs, f_ss, f_rs, qp_ss, qp_rs,
 ):
     dp = lax.axis_index("dp")
     me = lax.axis_index("cent")
@@ -55,8 +58,7 @@
         return 0
 
     lax.fori_loop(1, DP, sig_dp, 0)
-    own_copy = pltpu.make_async_copy(p_ref, G.at[z, x], loc)
-    own_copy.start()
+    G[z, x] = p_ref[...]
     qs[...] = jnp.zeros_like(qs)
     qs[0:4, :] = q_ref[...].astype(F32)
     qr[dp] = qs[...]
@@ -74,31 +76,141 @@
 
     lax.fori_loop(1, DP, q_send, 0)
 
-    def g_copy(o, xs, zs):
-        peer = (me + o) % CENT
-        return rcopy(p_ref, G.at[zs, xs], g_ss.at[o], g_rs.at[zs, xs], (dp, peer))
-
-    def g_send(o, _):
-        g_copy(o, x, z).start()
-        return 0
-
-    lax.fori_loop(1, CENT, g_send, 0)
+    def zdev(step):
+        return (dp, x * NZ + (z + NZ + step) % NZ)
+
+    def xdev(step):
+        return (dp, ((x + NX + step) % NX) * NZ + z)
+
+    STEP = (1, -1)
+
+    def a_z(zs, side, part=None):
+        lo, n = (0, D) if part is None else (part * HD, HD)
+        ref = G.at[zs, x, pl.ds(0, RA), pl.ds(lo, n)]
+        return rcopy(ref, ref, az_ss.at[zs, side], az_rs.at[zs if part != 1 else NZ], zdev(STEP[side]))
+
+    def b_z(zs, side, part=None):
+        lo, n = (0, NX) if part is None else (part * (NX // 2), NX // 2)
+        ref = G.at[zs, pl.ds(lo, n), pl.ds(RA, RB)]
+        return rcopy(ref, ref, bz_ss.at[zs, side], bz_rs.at[zs if part != 1 else NZ], zdev(STEP[side]))
+
+    def a_x(zs, xs, side):
+        ref = G.at[zs, xs, pl.ds(0, RA)]
+        return rcopy(ref, ref, ax_ss.at[zs, side], ax_rs.at[zs, side], xdev(STEP[side]))
+
+    def a_x2(zs, xs, side):
+        ref = G.at[zs, xs, pl.ds(0, RA), pl.ds(side * HD, HD)]
+        return rcopy(ref, ref, ax_ss.at[zs, 2 + side], ax_rs.at[zs, 2 + side], xdev(STEP[side]))
+
+    def b_x(xs, side):
+        ref = G.at[z, xs, pl.ds(RA, RB)]
+        return rcopy(ref, ref, bx_ss.at[side], bx_rs.at[side], xdev(STEP[side]))
+
+    def b_x2(xs, side):
+        ref = G.at[z, xs, pl.ds(RA, RB), pl.ds(side * HD, HD)]
+        return rcopy(ref, ref, bx_ss.at[2 + side], bx_rs.at[2 + side], xdev(STEP[side]))
+
+    def xfrom(side, n=1):
+        return (x + NX - n * STEP[side]) % NX
+
+    def zfrom(side, n):
+        return (z + NZ - n * STEP[side]) % NZ
+
+    def send_ax(zs):
+        for side in range(2):
+            a_x(zs, x, side).start()
+
+    def hop_ax(zs):
+        for side in range(2):
+            a_x(zs, xfrom(side), side).wait_recv()
+            a_x2(zs, xfrom(side), side).start()
+
+    def end_ax(zs):
+        for side in range(2):
+            a_x2(zs, xfrom(side, 2), side).wait_recv()
+
+    def take_a(d):
+        for side in range(2):
+            zs = zfrom(side, d)
+            if d < 4:
+                a_z(zs, side).wait_recv()
+                a_z(zs, side, None if d < 3 else side).start()
+                send_ax(zs)
+            else:
+                a_z(zs, side, side).wait_recv()
+        if d == 4:
+            send_ax(zfrom(0, 4))
+
+    def take_b(d):
+        for side in range(2):
+            zs = zfrom(side, d)
+            if d < 4:
+                b_z(zs, side).wait_recv()
+                b_z(zs, side, None if d < 3 else side).start()
+            else:
+                b_z(zs, side, side).wait_recv()
+
+    def gather(compute):
+        for side in range(2):
+            a_z(z, side).start()
+        for side in range(2):
+            b_x(x, side).start()
+        send_ax(z)
+        early()
+        for side in range(2):
+            b_x(xfrom(side), side).wait_recv()
+            b_x2(xfrom(side), side).start()
+        for side in range(2):
+            b_x2(xfrom(side, 2), side).wait_recv()
+        for side in range(2):
+            b_z(z, side).start()
+        take_a(1)
+        hop_ax(z)
+        end_ax(z)
+        compute(0)
+        take_b(1)
+        for side in range(2):
+            hop_ax(zfrom(side, 1))
+        for d in range(2, 5):
+            take_a(d)
+            for side in range(2):
+                end_ax(zfrom(side, d - 1))
+            compute(d - 1)
+            take_b(d)
+            for side in range(2 if d < 4 else 1):
+                hop_ax(zfrom(side, d))
+        end_ax(zfrom(0, 4))
+        compute(4)
+
+    def gather_drain():
+        for side in range(2):
+            b_x(x, side).wait_send()
+            b_x2(xfrom(side), side).wait_send()
+            for d in range(4):
+                zs = zfrom(side, d)
+                a_z(zs, side, None if d < 3 else side).wait_send()
+                b_z(zs, side, None if d < 3 else side).wait_send()
+
+        def w(zs, _):
+            for side in range(2):
+                a_x(zs, x, side).wait_send()
+                a_x2(zs, xfrom(side), side).wait_send()
+            return 0
+
+        lax.fori_loop(0, NZ, w, 0)
 
     def q_wait(o, _):
         q_copy(o, (dp + DP - o) % DP).wait_recv()
         return 0
 
-    lax.fori_loop(1, DP, q_wait, 0)
-    CQ[KL:KL + QP, :] = qr[...].reshape(QP, D).astype(BF16)
-    own_copy.wait()
+    def early():
+        lax.fori_loop(1, DP, q_wait, 0)
+        CQ[KL:KL + QP, :] = qr[...].reshape(QP, D).astype(BF16)
 
     def column(k):
         d = (k + 1) // 2
         sgn = 1 - 2 * (k % 2)
         return (z + NZ + sgn * d) % NZ
-
-    def g_wait(zc, xc):
-        g_copy(1, xc, zc).wait_recv()
 
     def st_copy(it, xc, zc, xs, zs):
         return rcopy(
@@ -121,23 +233,37 @@
         if it == 0:
             S[zc] = dots[KL:KL + QP, :] * sharpness
 
-    def softmax_pass(it, lhs_of):
-        if it == 0:
-            for i in range(1, NX):
-                g_wait(z, (x + i) % NX)
-        logits(it, z, lhs_of())
+    def own_column(it, lhs):
+        logits(it, z, lhs)
         st_r[it, z, x] = st_s[z, x]
         for i in range(1, NX):
             st_copy(it, (x + i) % NX, z, x, z).start()
 
+    def other_column(it, zc, lhs):
+        logits(it, zc, lhs)
+        for xc in range(NX):
+            st_copy(it, xc, zc, x, z).start()
+
+    def softmax_first():
+        def compute(d):
+            if d == 0:
+                own_column(0, CQ[...])
+            elif d == 4:
+                other_column(0, zfrom(0, 4), CQ[...])
+            else:
+                def side_step(i, _):
+                    other_column(0, (z + NZ + (2 * i - 1) * d) % NZ, CQ[...])
+                    return 0
+
+                lax.fori_loop(0, 2, side_step, 0)
+
+        gather(compute)
+
+    def softmax_second():
+        own_column(1, C2[...])
+
         def col_step(k, _):
-            zc = column(k)
-            if it == 0:
-                for xc in range(NX):
-                    g_wait(zc, xc)
-            logits(it, zc, lhs_of())
-            for xc in range(NX):
-                st_copy(it, xc, zc, x, z).start()
+            other_column(1, column(k), C2[...])
             return 0
 
         lax.fori_loop(1, NZ, col_step, 0)
@@ -326,34 +452,75 @@
         for c in fw:
             c.wait_send()
 
-    softmax_pass(0, lambda: CQ[...])
+    def finish():
+        if STOP >= 0:
+            gather_drain()
+
+        def wsq(o, _):
+            q_copy(o, dp).wait_send()
+            return 0
+
+        lax.fori_loop(1, DP, wsq, 0)
+        if STOP < 90:
+            out_ref[...] = jnp.zeros_like(out_ref)
+            loss_ref[...] = jnp.zeros_like(loss_ref)
+
+    def drain(it):
+        def ws(o, _):
+            dst = (me + o) % CENT
+            st_copy(it, dst // NZ, dst % NZ, x, z).wait_send()
+            rs_copy(it, o, x, z).wait_send()
+            rs_copy(it, o, dst // NZ, dst % NZ).wait_recv()
+            return 0
+
+        lax.fori_loop(1, CENT, ws, 0)
+
+    if STOP == 0:
+        gather(lambda d: None)
+        return finish()
+    if STOP == -1:
+        early()
+        return finish()
+    softmax_first()
     owner_combine(0)
+    if STOP == 1:
+        drain(0)
+        return finish()
     query_post()
+    if STOP == 2:
+        drain(0)
+        query_finish()
+        return finish()
     numer_pass(0)
+    if STOP == 3:
+        query_finish()
+        return finish()
     newc = reduce_dp(0)
     own[...] = newc
     C2[pl.ds(myrow, 32), :] = newc.astype(BF16)
     NB[1, pl.ds(myrow, 32), :] = jnp.broadcast_to(jnp.sum(newc * newc, axis=1, keepdims=True), (32, 128))
+    if STOP == 4:
+        query_finish()
+        return finish()
     all_gather_rows([C2, NB.at[1]], c_ss, c_rs)
-
-    softmax_pass(1, lambda: C2[...])
+    if STOP == 5:
+        query_finish()
+        return finish()
+
+    softmax_second()
     owner_combine(1)
     query_finish()
+    if STOP == 6:
+        drain(1)
+        return finish()
     numer_pass(1)
+    if STOP == 7:
+        return finish()
     out_ref[pl.ds(myrow, 32), :] = reduce_dp(1)
+    if STOP == 8:
+        return finish()
     all_gather_rows([out_ref], f_ss, f_rs)
-
-    def ws(o, _):
-        g_copy(o, x, z).wait_send()
-        return 0
-
-    lax.fori_loop(1, CENT, ws, 0)
-
-    def wsq(o, _):
-        q_copy(o, dp).wait_send()
-        return 0
-
-    lax.fori_loop(1, DP, wsq, 0)
+    finish()
 
 
 def on_device(passages, queries, init_centroids, pattern, positive_offset):
@@ -386,7 +553,8 @@
             pltpu.VMEM((DP, 8, D), F32),
             pltpu.VMEM((DP, 8, 128), F32),
             pltpu.VMEM((DP, 8, 128), F32),
-            dma((CENT,)), dma((NZ, NX)),
+            dma((NZ, 2)), dma((NZ + 1,)), dma((NZ, 2)), dma((NZ + 1,)),
+            dma((NZ, 4)), dma((NZ, 4)), dma((4,)), dma((4,)),
             dma((DP,)), dma((DP,)),
             dma((NZ, NX)), dma((2, NZ, NX)),
             dma((2, CENT)), dma((2, NZ, NX)),
@@ -394,7 +562,6 @@
             dma((2, 8)), dma((2, 8)),
             dma((1, 8)), dma((1, 8)),
             dma((DP,)), dma((DP,)),
-            dma,
         ],
         compiler_params=pltpu.CompilerParams(
             collective_id=0, has_side_effects=True, vmem_limit_bytes=40 * 1024 * 1024

time: 250 us -> 132 us (0.53)
  Pallas kernels: 244 us -> 127 us
    pallas_call x1, Pallas kernels: 244 us -> 127 us  [on_device(): pl.pallas_call(kernel, out_shape=(jax.ShapeDtypeStruct((KL, D), F32), jax...]
where the time goes in v2:
time: 132 us
  Pallas kernels  127 us (96%)
  local copies, waits for them, and re-layouts  4.73 us (4%)
    pallas_call x1, Pallas kernels, on_device(): pl.pallas_call(kernel, out_shape=(jax.ShapeDtypeStruct((KL, D), F32), jax...  127 us
    unnamed x11, local copies, waits for them, and re-layouts  2.72 us

profile of v2, /device:TPU:1, one launch (start us, length us, event | category | flops | bytes accessed | tf_op | source)
XLA Modules:
  0.0 132.3 jit_solution(12154881062405411760)
XLA Ops:
  0.6 0.0 copy-start.4
  0.6 0.7 copy-done.4
  1.3 0.0 copy-start.3
  1.3 0.1 concatenate.9
  1.5 0.0 copy-start
  1.5 0.1 copy.11
  1.6 0.5 copy-done.3
  2.0 0.5 concatenate.8
  2.6 0.3 copy.10
  2.9 0.0 copy-start.1
  2.9 0.1 dynamic-slice_add_fusion
  3.0 0.3 copy.15
  3.3 0.0 copy-start.2
  3.3 0.0 copy-done
  3.3 0.5 copy-done.1
  3.8 0.2 copy-done.2
  4.0 126.8 %shard_map.68 = (f32[256,768]{1,0:T(8,128)S(1)}, f32[8,128]{1,0:T(8,128)S(1)}) custom-call(bf16[128,768]{1,0:T(8,128)(2,1)S(1)} %copy-done.1, bf16[4,768]{1,0:T(4,128)(2,1)S(1)} %copy-done.2, f32[256,768]{1,0:T(8,128)S(1)} %copy-done, s32[64,128]{1,0:T(8,128)S(1)} %pad_bitcast_fusion.meta_ref), custom_call_target="tpu_custom_call" | custom-call | tf_op jit(solution)/shard_map/pallas_call | solution.py:533
  130.8 0.6 slice_reduce_fusion
  131.4 0.9 copy.17
  (1 shorter events, 0.0 us)
Async XLA Ops:
  0.6 0.7 copy-start.4
  1.3 0.7 copy-start.3
  1.5 1.8 %copy-start = (f32[256,768]{1,0:T(8,128)S(1)}, f32[256,768]{1,0:T(8,128)}, u32[]{:S(2)}) copy-start(f32[256,768]{1,0:T(8,128)} %c_ref.1) | copy-start | bytes 2359300
  2.9 0.9 copy-start.1
  3.3 0.7 copy-start.2

commit v3 on v2

v3 whole, which is shorter than its diff:
```python
import jax
import jax.numpy as jnp
from jax import lax
from jax.experimental import pallas as pl
from jax.experimental.pallas import tpu as pltpu
from jax.sharding import PartitionSpec as P

MESH = pl.DeviceIdType.MESH
BLOCK = 128
D = 768
HD = 384
NX, NZ, NY = 4, 8, 4
CENT = NX * NZ
DP = 2 * NY
KL = 256
QP = 64
W = D + 128
CH = 2
RC = KL // CH
RH = RC // 2
RQ = RH // NY
sharpness = 0.05
NEG = -1e30
STOP = 99
RA = 80
RB = 128 - RA
NARROW = (True, False)
F32 = jnp.float32
BF16 = jnp.bfloat16


def rcopy(src, dst, ss, rs, dev):
    return pltpu.make_async_remote_copy(
        src_ref=src, dst_ref=dst, send_sem=ss, recv_sem=rs, device_id=dev, device_id_type=MESH
    )


def three(v, rows):
    lane = lax.broadcasted_iota(jnp.int32, (rows, 128), 1)
    v = jnp.broadcast_to(v, (rows, 128))
    hi = v.astype(BF16).astype(F32)
    mid = (v - hi).astype(BF16).astype(F32)
    lo = v - hi - mid
    return jnp.where(lane == 0, hi, jnp.where(lane == 1, mid, jnp.where(lane == 2, lo, 0.0))).astype(BF16)


def kernel(
    p_ref, q_ref, c_ref, pat_ref, off_ref, out_ref, loss_ref,
    G, E, S, CQ, C2, NB, acc, rb1, nar, rb2n, rb2, own, cv, qv, patv, offv, patb, ml, sl, st_s, st_r, rs_r,
    qs, qr, qp_s, qp_r,
    az_ss, az_rs, bz_ss, bz_rs, ax_ss, ax_rs, bx_ss, bx_rs, q_ss, q_rs, st_ss, st_rs, rs_ss, rs_rs,
    n1_ss, n1_rs, n2_ss, n2_rs, c_ss, c_rs, qp_ss, qp_rs, loc,
):
    dp = lax.axis_index("dp")
    me = lax.axis_index("cent")
    x, z = me // NZ, me % NZ
    y, core = dp // 2, dp % 2
    sib = (dp + 1 - 2 * core, me)

    def cdev(xx, zz):
        return (dp, xx * NZ + zz)

    loads = [
        pltpu.make_async_copy(src, dst, loc.at[i])
        for i, (src, dst) in enumerate(
            [(p_ref, G.at[z, x]), (q_ref, qv), (c_ref, cv), (pat_ref, patv), (off_ref, offv)]
        )
    ]
    for cp in loads:
        cp.start()

    barrier = pltpu.get_barrier_semaphore()
    for dev in (
        cdev(x, (z + 1) % NZ), cdev(x, (z + NZ - 1) % NZ),
        cdev((x + 1) % NX, z), cdev((x + 2) % NX, z), cdev((x + 3) % NX, z),
    ):
        pl.semaphore_signal(barrier, inc=1, device_id=dev, device_id_type=MESH)
    for o in range(1, DP):
        pl.semaphore_signal(barrier, inc=1, device_id=((dp + o) % DP, me), device_id_type=MESH)
    loads[1].wait()
    qs[...] = jnp.zeros_like(qs)
    qs[0:4, :] = qv[...].astype(F32)
    qr[dp] = qs[...]
    loads[0].wait()
    pl.semaphore_wait(barrier, 5 + DP - 1)

    def q_copy(o, src):
        return rcopy(qs, qr.at[src], q_ss.at[o], q_rs.at[src], ((dp + o) % DP, me))

    def zdev(step):
        return (dp, x * NZ + (z + NZ + step) % NZ)

    def xdev(step):
        return (dp, ((x + NX + step) % NX) * NZ + z)

    STEP = (1, -1)

    def a_z(zs, side, part=None):
        lo, n = (0, D) if part is None else (part * HD, HD)
        ref = G.at[zs, x, pl.ds(0, RA), pl.ds(lo, n)]
        return rcopy(ref, ref, az_ss.at[zs, side], az_rs.at[zs if part != 1 else NZ], zdev(STEP[side]))

    def b_z(zs, side, part):
        ref = G.at[zs, pl.ds(part * (NX // 2), NX // 2), pl.ds(RA, RB)]
        return rcopy(ref, ref, bz_ss.at[zs, side, part], bz_rs.at[zs, part], zdev(STEP[side]))

    def a_x(zs, xs, side):
        ref = G.at[zs, xs, pl.ds(0, RA)]
        return rcopy(ref, ref, ax_ss.at[zs, side], ax_rs.at[zs, side], xdev(STEP[side]))

    def a_x2(zs, xs, side):
        ref = G.at[zs, xs, pl.ds(0, RA), pl.ds(side * HD, HD)]
        return rcopy(ref, ref, ax_ss.at[zs, 2 + side], ax_rs.at[zs, 2 + side], xdev(STEP[side]))

    def b_x(xs, i):
        ref = G.at[z, xs, pl.ds(RA, RB)]
        return rcopy(ref, ref, bx_ss.at[i], bx_rs.at[i], xdev(i))

    def xfrom(side, n=1):
        return (x + NX - n * STEP[side]) % NX

    def zfrom(side, n):
        return (z + NZ - n * STEP[side]) % NZ

    def send_ax(zs):
        for side in range(2):
            a_x(zs, x, side).start()

    def hop_ax(zs):
        for side in range(2):
            a_x(zs, xfrom(side), side).wait_recv()
            a_x2(zs, xfrom(side), side).start()

    def end_ax(zs):
        for side in range(2):
            a_x2(zs, xfrom(side, 2), side).wait_recv()

    def take_a(d):
        for side in range(2):
            zs = zfrom(side, d)
            if d < 4:
                a_z(zs, side).wait_recv()
                a_z(zs, side, None if d < 3 else side).start()
                send_ax(zs)
            else:
                a_z(zs, side, side).wait_recv()
        if d == 4:
            send_ax(zfrom(0, 4))

    def take_b(d):
        for part in range(2):
            for side in range(2):
                zs = zfrom(side, d)
                if d < 4:
                    b_z(zs, side, part).wait_recv()
                    if d < 3 or part == side:
                        b_z(zs, side, part).start()
                elif part == side:
                    b_z(zs, side, part).wait_recv()

    def hop(d):
        for side in range(2 if 0 < d < 4 else 1):
            hop_ax(zfrom(side, d))

    def end(d):
        for side in range(2 if 0 < d < 4 else 1):
            end_ax(zfrom(side, d))

    def gather(compute):
        for side in range(2):
            a_z(z, side).start()
        for i in (2, 1, 3):
            b_x(x, i).start()
        send_ax(z)
        for o in range(1, DP):
            q_copy(o, dp).start()
        take_a(1)
        for i in (1, 3, 2):
            b_x((x + NX - i) % NX, i).wait_recv()
        for part in range(2):
            for side in range(2):
                b_z(z, side, part).start()
        hop(0)
        take_a(2)
        early()
        for d in range(5):
            if d < 4:
                hop(d + 1)
                take_b(d + 1)
            end(d)
            compute(d)
            if d < 2:
                take_a(d + 3)

    def gather_drain():
        for i in range(1, NX):
            b_x(x, i).wait_send()
        for side in range(2):
            for d in range(4):
                zs = zfrom(side, d)
                a_z(zs, side, None if d < 3 else side).wait_send()
                for part in range(2):
                    if d < 3 or part == side:
                        b_z(zs, side, part).wait_send()

        def w(zs, _):
            for side in range(2):
                a_x(zs, x, side).wait_send()
                a_x2(zs, xfrom(side), side).wait_send()
            return 0

        lax.fori_loop(0, NZ, w, 0)

    def q_wait(o, _):
        q_copy(o, (dp + DP - o) % DP).wait_recv()
        return 0

    def early():
        for i in range(2, 5):
            loads[i].wait()
        acc[...] = jnp.zeros_like(acc)
        c0 = cv[...]
        CQ[0:KL, :] = c0.astype(BF16)
        NB[...] = jnp.broadcast_to(jnp.sum(c0 * c0, axis=1, keepdims=True), (KL, 128))
        lane = lax.broadcasted_iota(jnp.int32, (8, BLOCK), 1)
        sub = lax.broadcasted_iota(jnp.int32, (8, BLOCK), 0)
        pick = (lane == me * 4 + sub) & (sub < 4)
        for j in range(DP):
            for i in range(5):
                row = patv[i:i + 1, j * BLOCK:(j + 1) * BLOCK] if i < 4 else offv[j:j + 1, :]
                vals = jnp.where(pick, jnp.broadcast_to(row.astype(F32), (8, BLOCK)), 0.0)
                patb[i, 8 * j:8 * j + 8, :] = jnp.broadcast_to(jnp.sum(vals, axis=1, keepdims=True), (8, BLOCK))
        lax.fori_loop(1, DP, q_wait, 0)
        CQ[KL:KL + QP, :] = qr[...].reshape(QP, D).astype(BF16)

    def column(k):
        d = (k + 1) // 2
        sgn = 1 - 2 * (k % 2)
        return (z + NZ + sgn * d) % NZ

    def st_copy(it, xc, zc, xs, zs):
        return rcopy(
            st_s.at[zc, xc], st_r.at[it, zs, xs], st_ss.at[zc, xc], st_rs.at[it, zs, xs], cdev(xc, zc)
        )

    def logit_part(zc, dots, lo, n, h):
        nb = NB[lo:lo + n, :]
        for xc in range(NX):
            a = xc * BLOCK
            ll = sharpness * (2.0 * dots[0:n, a:a + BLOCK] - nb)
            m = jnp.max(ll, axis=0, keepdims=True)
            e = jnp.exp(ll - m)
            E[zc, lo:lo + n, a:a + BLOCK] = e
            ml[zc, h:h + 1, a:a + BLOCK] = m
            sl[zc, h:h + 1, a:a + BLOCK] = jnp.sum(e, axis=0, keepdims=True)

    def dot_nt(lhs, rhs):
        return lax.dot_general(lhs, rhs, (((1,), (1,)), ((), ())), preferred_element_type=F32)

    def ship(it, zc, mine):
        if mine:
            st_r[it, z, x] = st_s[z, x]
            for i in range(1, NX):
                st_copy(it, (x + i) % NX, z, x, z).start()
        else:
            for xc in range(NX):
                st_copy(it, xc, zc, x, z).start()

    def first_column(zc, mine):
        dots = dot_nt(CQ[...], G[zc].reshape(NX * BLOCK, D))
        logit_part(zc, dots, 0, KL, 0)
        S[zc] = dots[KL:KL + QP, :] * sharpness
        m = ml[zc, 0:1, :]
        s = sl[zc, 0:1, :]
        ml[zc, 1:2, :] = m
        for xc in range(NX):
            st_s[zc, xc, 0:1, :] = m[:, xc * BLOCK:(xc + 1) * BLOCK]
            st_s[zc, xc, 1:2, :] = s[:, xc * BLOCK:(xc + 1) * BLOCK]
        ship(0, zc, mine)

    def softmax_first():
        def compute(d):
            if d == 0:
                first_column(z, True)
            elif d == 4:
                first_column(zfrom(0, 4), False)
            else:
                def side_step(i, _):
                    first_column((z + NZ + (2 * i - 1) * d) % NZ, False)
                    return 0

                lax.fori_loop(0, 2, side_step, 0)

        gather(compute)

    def second_column(zc, h):
        dots = dot_nt(C2[h * RC:(h + 1) * RC, 0:D], G[zc].reshape(NX * BLOCK, D))
        logit_part(zc, dots, h * RC, RC, h)

    def second_ship(zc, mine):
        for xc in range(NX):
            a = xc * BLOCK
            ma, mb = ml[zc, 0:1, a:a + BLOCK], ml[zc, 1:2, a:a + BLOCK]
            m = jnp.maximum(ma, mb)
            st_s[zc, xc, 0:1, :] = m
            st_s[zc, xc, 1:2, :] = (
                sl[zc, 0:1, a:a + BLOCK] * jnp.exp(ma - m) + sl[zc, 1:2, a:a + BLOCK] * jnp.exp(mb - m)
            )
        ship(1, zc, mine)

    def softmax_second():
        for h in range(CH):
            rows_wait(0, h)
            rows = slice(h * RC, (h + 1) * RC)
            NB[rows, :] = jnp.broadcast_to(
                jnp.sum(C2[rows, D:W].astype(F32), axis=1, keepdims=True), (RC, 128)
            )
            if h < CH - 1:
                def part(zc, _):
                    second_column(zc, h)
                    return 0

                lax.fori_loop(0, NZ, part, 0)
            else:
                def last(k, _):
                    zc = column(k)
                    second_column(zc, h)
                    second_ship(zc, False)
                    return 0

                second_column(z, h)
                second_ship(z, True)
                lax.fori_loop(1, NZ, last, 0)

    def rs_copy(it, o, xo, zo):
        peer = (me + o) % CENT
        return rcopy(
            rs_r.at[it, z, x], rs_r.at[it, zo, xo], rs_ss.at[it, o], rs_rs.at[it, zo, xo], (dp, peer)
        )

    def owner_combine(it):
        def w(o, _):
            src = (me + o) % CENT
            st_copy(it, x, z, src // NZ, src % NZ).wait_recv()
            return 0

        lax.fori_loop(1, CENT, w, 0)
        m = st_r[it, :, :, 0:1, :].reshape(CENT, 1, BLOCK)
        s = st_r[it, :, :, 1:2, :].reshape(CENT, 1, BLOCK)
        top = jnp.max(m, axis=0)
        tot = jnp.sum(s * jnp.exp(m - top[None]), axis=0)
        rs_r[it, z, x, 0:1, :] = top
        rs_r[it, z, x, 1:2, :] = 1.0 / tot

        def snd(o, _):
            rs_copy(it, o, x, z).start()
            return 0

        lax.fori_loop(1, CENT, snd, 0)

    def query_post():
        pats = [patb[i] for i in range(4)]
        off = patb[4]
        lane = lax.broadcasted_iota(jnp.int32, (QP, BLOCK), 1)
        lanef = lane.astype(F32)

        def allow_of(b):
            return (pats[0] == b) | (pats[1] == b) | (pats[2] == b) | (pats[3] == b)

        def p1(zc, mx):
            for xc in range(NX):
                b = (dp * CENT + xc * NZ + zc).astype(F32)
                sv = S[zc, :, xc * BLOCK:(xc + 1) * BLOCK]
                mx = jnp.maximum(mx, jnp.where(allow_of(b), sv, NEG))
            return mx

        mx = lax.fori_loop(0, NZ, p1, jnp.full((QP, BLOCK), NEG, F32))
        mrow = jnp.max(mx, axis=1, keepdims=True)
        mb = jnp.broadcast_to(mrow, (QP, BLOCK))

        def p2(zc, carry):
            tot, pos = carry
            for xc in range(NX):
                b = (dp * CENT + xc * NZ + zc).astype(F32)
                sv = S[zc, :, xc * BLOCK:(xc + 1) * BLOCK]
                tot = tot + jnp.where(allow_of(b), jnp.exp(sv - mb), 0.0)
                pos = pos + jnp.where((pats[0] == b) & (lanef == off), sv, 0.0)
            return tot, pos

        zero = jnp.zeros((QP, BLOCK), F32)
        tot, pos = lax.fori_loop(0, NZ, p2, (zero, zero))
        trow = jnp.broadcast_to(jnp.sum(tot, axis=1, keepdims=True), (QP, BLOCK))
        prow = jnp.broadcast_to(jnp.sum(pos, axis=1, keepdims=True), (QP, BLOCK))
        packed = jnp.where(lane == 0, mb, jnp.where(lane == 1, trow, prow))
        qp_s[...] = packed.reshape(DP, 8, BLOCK)
        qp_r[dp] = qp_s[dp]

        def snd(o, _):
            qp_copy(o, (dp + o) % DP, dp).start()
            return 0

        lax.fori_loop(1, DP, snd, 0)

    def qp_copy(o, dst, src):
        return rcopy(qp_s.at[dst], qp_r.at[src], qp_ss.at[o], qp_rs.at[src], (dst, me))

    def query_finish():
        def w(o, _):
            qp_copy(o, (dp + o) % DP, (dp + o) % DP).wait_recv()
            return 0

        lax.fori_loop(1, DP, w, 0)
        m = qp_r[:, :, 0:1]
        t = qp_r[:, :, 1:2]
        p = qp_r[:, :, 2:3]
        top = jnp.max(m, axis=0)
        tot = jnp.sum(t * jnp.exp(m - top[None]), axis=0)
        ps = jnp.sum(p, axis=0)
        loss = jnp.broadcast_to(jnp.log(tot) + top - ps, (8, BLOCK))
        lane = lax.broadcasted_iota(jnp.int32, (8, BLOCK), 1)
        sub = lax.broadcasted_iota(jnp.int32, (8, BLOCK), 0)
        loss_ref[...] = jnp.sum(jnp.where(lane == sub, loss, 0.0), axis=0, keepdims=True)[:, 0:4]

        def ws(o, _):
            qp_copy(o, (dp + o) % DP, dp).wait_send()
            return 0

        lax.fori_loop(1, DP, ws, 0)

    def stats_wait(it):
        def w(o, _):
            src = (me + o) % CENT
            rs_copy(it, o, src // NZ, src % NZ).wait_recv()
            return 0

        lax.fori_loop(1, CENT, w, 0)

    def stats_drain(it):
        def ws(o, _):
            dst = (me + o) % CENT
            st_copy(it, dst // NZ, dst % NZ, x, z).wait_send()
            rs_copy(it, o, x, z).wait_send()
            return 0

        lax.fori_loop(1, CENT, ws, 0)

    def numer(it, h, lo, hi):
        rows = slice(h * RC, (h + 1) * RC)

        def col(zc, _):
            cnt = acc[it, rows, D:W]
            parts = []
            for xc in range(NX):
                a = xc * BLOCK
                g = jnp.exp(ml[zc, h:h + 1, a:a + BLOCK] - rs_r[it, zc, xc, 0:1, :]) * rs_r[it, zc, xc, 1:2, :]
                r = E[zc, rows, a:a + BLOCK] * g
                cnt = cnt + r
                parts.append(r.astype(BF16))
            acc[it, rows, D:W] = cnt
            r_all = jnp.concatenate(parts, axis=1)
            acc[it, rows, 0:D] += jnp.dot(r_all, G[zc].reshape(NX * BLOCK, D), preferred_element_type=F32)
            return 0

        lax.fori_loop(lo, hi, col, 0)

    mine_at = [pl.multiple_of(h * RC + core * RH, RH) for h in range(CH)]
    theirs_at = [pl.multiple_of(h * RC + RH - core * RH, RH) for h in range(CH)]

    def pair_copy(it, h):
        return rcopy(acc.at[it, pl.ds(theirs_at[h], RH)], rb1.at[it, h], n1_ss.at[it, h], n1_rs.at[it, h], sib)

    def quarter(h, yy):
        return pl.ds(pl.multiple_of(h * RC + core * RH + yy * RQ, RQ), RQ)

    def y_copy(it, h, i):
        yp = (y + i) % NY
        sem = (n2_ss.at[it, h, i], n2_rs.at[it, h, i])
        if NARROW[it]:
            src = nar.at[it, h, pl.ds(pl.multiple_of(yp * RQ, RQ), RQ)]
            return rcopy(src, rb2n.at[it, h, i], *sem, (yp * 2 + core, me))
        return rcopy(acc.at[it, quarter(h, yp)], rb2.at[it, h, i], *sem, (yp * 2 + core, me))

    def pair_sum(it, h):
        pair_copy(it, h).wait_recv()
        tot = acc[it, pl.ds(mine_at[h], RH), :] + rb1[it, h]
        acc[it, pl.ds(mine_at[h], RH), :] = tot
        if NARROW[it]:
            nar[it, h, :, 0:D] = tot[:, 0:D].astype(BF16)
            nar[it, h, :, D:W] = three(jnp.sum(tot[:, D:W], axis=1, keepdims=True), RH)
        for i in (2, 1, 3):
            y_copy(it, h, i).start()

    def update(it, h):
        tot = acc[it, quarter(h, y), :]
        for i in (1, 3, 2):
            y_copy(it, h, i).wait_recv()
            tot = tot + (rb2n[it, h, i].astype(F32) if NARROW[it] else rb2[it, h, i])
        counts = jnp.sum(tot[:, D:W], axis=1, keepdims=True)
        cold = cv[quarter(h, y), :] if it == 0 else own[h]
        return (tot[:, 0:D] + cold) / (counts + 1.0)

    def row_copy(k, h, i):
        arr = C2 if k == 0 else out_ref
        ref = arr.at[quarter(h, y)]
        return rcopy(ref, ref, c_ss.at[k, h, i], c_rs.at[k, h, i], (((y + i) % NY) * 2 + core, me))

    def half_copy(k, h):
        arr = C2 if k == 0 else out_ref
        ref = arr.at[pl.ds(mine_at[h], RH)]
        return rcopy(ref, ref, c_ss.at[k, h, 0], c_rs.at[k, h, 0], sib)

    def rows_send(k, h):
        for i in (2, 1, 3):
            row_copy(k, h, i).start()

    def rows_pass(k, h):
        for i in (1, 3, 2):
            row_copy(k, h, i).wait_recv()
        half_copy(k, h).start()

    def rows_wait(k, h):
        half_copy(k, h).wait_recv()

    def reduce_drain(it):
        for h in range(CH):
            pair_copy(it, h).wait_send()
            for i in range(1, NY):
                y_copy(it, h, i).wait_send()
                row_copy(it, h, i).wait_send()
            half_copy(it, h).wait_send()

    def finish():
        if STOP >= 0:
            gather_drain()

        def wsq(o, _):
            q_copy(o, dp).wait_send()
            return 0

        lax.fori_loop(1, DP, wsq, 0)
        if STOP < 90:
            out_ref[...] = jnp.zeros_like(out_ref)
            loss_ref[...] = jnp.zeros_like(loss_ref)

    def mid(it):
        numer(it, 0, 0, NZ)
        pair_copy(it, 0).start()
        numer(it, 1, 0, NZ // 2)
        pair_sum(it, 0)
        numer(it, 1, NZ // 2, NZ)
        pair_copy(it, 1).start()
        pair_sum(it, 1)

    if STOP == -2:
        for o in range(1, DP):
            q_copy(o, dp).start()
        lax.fori_loop(1, DP, q_wait, 0)
        for i in range(2, 5):
            loads[i].wait()
        return finish()
    if STOP == -1:
        for o in range(1, DP):
            q_copy(o, dp).start()
        early()
        return finish()
    if STOP == 0:
        gather(lambda d: None)
        return finish()
    softmax_first()
    owner_combine(0)
    if STOP == 1:
        stats_wait(0)
        stats_drain(0)
        return finish()
    query_post()
    stats_wait(0)
    if STOP == 2:
        stats_drain(0)
        query_finish()
        return finish()
    mid(0)
    for h in range(CH):
        newc = update(0, h)
        own[h] = newc
        C2[quarter(h, y), 0:D] = newc.astype(BF16)
        C2[quarter(h, y), D:W] = three(jnp.sum(newc * newc, axis=1, keepdims=True), RQ)
        rows_send(0, h)
    stats_drain(0)
    for h in range(CH):
        rows_pass(0, h)
    if STOP == 5:
        for h in range(CH):
            rows_wait(0, h)
        reduce_drain(0)
        query_finish()
        return finish()

    softmax_second()
    owner_combine(1)
    query_finish()
    stats_wait(1)
    if STOP == 6:
        stats_drain(1)
        reduce_drain(0)
        return finish()
    mid(1)
    for h in range(CH):
        out_ref[quarter(h, y), :] = update(1, h).astype(BF16)
        rows_send(1, h)
    stats_drain(1)
    reduce_drain(0)
    for h in range(CH):
        rows_pass(1, h)
    for h in range(CH):
        rows_wait(1, h)
    reduce_drain(1)
    finish()


def on_device(passages, queries, init_centroids, pattern, positive_offset):
    vm = pl.BlockSpec(memory_space=pltpu.VMEM)
    anywhere = pl.BlockSpec(memory_space=pl.ANY)
    dma = pltpu.SemaphoreType.DMA
    centroids, loss = pl.pallas_call(
        kernel,
        out_shape=(jax.ShapeDtypeStruct((KL, D), BF16), jax.ShapeDtypeStruct((1, 4), F32)),
        in_specs=[anywhere] * 5,
        out_specs=(vm, vm),
        scratch_shapes=[
            pltpu.VMEM((NZ, NX, BLOCK, D), BF16),
            pltpu.VMEM((NZ, KL, NX * BLOCK), F32),
            pltpu.VMEM((NZ, QP, NX * BLOCK), F32),
            pltpu.VMEM((KL + QP, D), BF16),
            pltpu.VMEM((KL, W), BF16),
            pltpu.VMEM((KL, 128), F32),
            pltpu.VMEM((2, KL, W), F32),
            pltpu.VMEM((2, CH, RH, W), F32),
            pltpu.VMEM((2, CH, RH, W), BF16),
            pltpu.VMEM((2, CH, NY, RQ, W), BF16),
            pltpu.VMEM((2, CH, NY, RQ, W), F32),
            pltpu.VMEM((CH, RQ, D), F32),
            pltpu.VMEM((KL, D), F32),
            pltpu.VMEM((4, D), BF16),
            pltpu.VMEM((4, 1024), jnp.int32),
            pltpu.VMEM((DP, 128), jnp.int32),
            pltpu.VMEM((5, QP, 128), F32),
            pltpu.VMEM((NZ, CH, NX * BLOCK), F32),
            pltpu.VMEM((NZ, CH, NX * BLOCK), F32),
            pltpu.VMEM((NZ, NX, 2, 128), F32),
            pltpu.VMEM((2, NZ, NX, 2, 128), F32),
            pltpu.VMEM((2, NZ, NX, 2, 128), F32),
            pltpu.VMEM((8, D), F32),
            pltpu.VMEM((DP, 8, D), F32),
            pltpu.VMEM((DP, 8, 128), F32),
            pltpu.VMEM((DP, 8, 128), F32),
            dma((NZ, 2)), dma((NZ + 1,)), dma((NZ, 2, 2)), dma((NZ, 2)),
            dma((NZ, 4)), dma((NZ, 4)), dma((4,)), dma((4,)),
            dma((DP,)), dma((DP,)),
            dma((NZ, NX)), dma((2, NZ, NX)),
            dma((2, CENT)), dma((2, NZ, NX)),
            dma((2, CH)), dma((2, CH)),
            dma((2, CH, NY)), dma((2, CH, NY)),
            dma((2, CH, NY)), dma((2, CH, NY)),
            dma((DP,)), dma((DP,)),
            dma((5,)),
        ],
        compiler_params=pltpu.CompilerParams(
            collective_id=0, has_side_effects=True, vmem_limit_bytes=56 * 1024 * 1024
        ),
    )(passages, queries, init_centroids, pattern.T, positive_offset.reshape(DP, 128))
    return centroids.astype(F32), loss.reshape(4)


def solution(mesh):
    placed = (P(("dp", "cent"), None), P(("dp", "cent"), None), P("cent", None), P(), P())
    return jax.shard_map(
        on_device,
        mesh=mesh,
        in_specs=placed,
        out_specs=(P("cent", None), P(("dp", "cent"))),
        check_vma=False,
    )
```

time: 132 us -> 120 us (0.909)
  Pallas kernels: 127 us -> 117 us
  local copies, waits for them, and re-layouts: 4.73 us -> 0.52 us
  other arithmetic: 0.09 us -> 1.93 us
    pallas_call x1, Pallas kernels: 127 us -> 117 us  [on_device(): pl.pallas_call(kernel, out_shape=(jax.ShapeDtypeStruct((KL, D), BF16), ja...]
    unnamed x11 -> x3, local copies, waits for them, and re-layouts: 2.72 us -> 0.52 us
    convert_element_type x0 -> x1, other arithmetic: none -> 1.93 us  [on_device(): return (centroids.astype(F32), loss.reshape(4))]
where the time goes in v3:
time: 120 us
  Pallas kernels  117 us (98%)
  other arithmetic  1.93 us (2%)
    pallas_call x1, Pallas kernels, on_device(): pl.pallas_call(kernel, out_shape=(jax.ShapeDtypeStruct((KL, D), BF16), ja...  117 us

profile of v3, /device:TPU:1, one launch (start us, length us, event | category | flops | bytes accessed | tf_op | source)
XLA Modules:
  0.0 119.7 jit_solution(11415939970934060613)
XLA Ops:
  0.6 116.6 %shard_map.68 = (bf16[256,768]{1,0:T(8,128)(2,1)}, f32[1,4]{1,0:T(1,128)}) custom-call(bf16[128,768]{1,0:T(8,128)(2,1)} %p_ref.1, bf16[4,768]{1,0:T(4,128)(2,1)} %q_ref.1, f32[256,768]{1,0:T(8,128)} %c_ref.1, s32[4,1024]{1,0:T(4,128)} %bitcast.3, s32[8,128]{1,0:T(8,128)} %bitcast.4), custom_call_target="tpu_custom_call" | custom-call | tf_op jit(solution)/shard_map/pallas_call | solution.py:624
  117.3 0.0 copy-start
  117.3 1.9 %convert_element_type.3 = f32[256,768]{1,0:T(8,128)} convert(bf16[256,768]{1,0:T(8,128)(2,1)} %get-tuple-element.4) | non-fusion elementwise | flops 196608 | bytes 1179648 | tf_op jit(solution)/shard_map/convert_element_type | solution.py:671
  119.2 0.0 copy-done
  119.2 0.5 copy.8
Async XLA Ops:
  117.3 1.9 %copy-start = (f32[1,4]{1,0:T(1,128)S(1)}, f32[1,4]{1,0:T(1,128)}, u32[]{:S(2)}) copy-start(f32[1,4]{1,0:T(1,128)} %get-tuple-element.5) | copy-start | bytes 52

commit v4 on v3

--- a/solution.py
+++ b/solution.py
@@ -46,7 +46,7 @@
 
 def kernel(
     p_ref, q_ref, c_ref, pat_ref, off_ref, out_ref, loss_ref,
-    G, E, S, CQ, C2, NB, acc, rb1, nar, rb2n, rb2, own, cv, qv, patv, offv, patb, ml, sl, st_s, st_r, rs_r,
+    G, E, S, CQ, C2, NB, acc, rb1, nar, rb2n, rb2, own, cv, qv, patv, offv, patb, st_s, st_r, rs_r,
     qs, qr, qp_s, qp_r,
     az_ss, az_rs, bz_ss, bz_rs, ax_ss, ax_rs, bx_ss, bx_rs, q_ss, q_rs, st_ss, st_rs, rs_ss, rs_rs,
     n1_ss, n1_rs, n2_ss, n2_rs, c_ss, c_rs, qp_ss, qp_rs, loc,
@@ -147,16 +147,15 @@
         if d == 4:
             send_ax(zfrom(0, 4))
 
-    def take_b(d):
-        for part in range(2):
-            for side in range(2):
-                zs = zfrom(side, d)
-                if d < 4:
-                    b_z(zs, side, part).wait_recv()
-                    if d < 3 or part == side:
-                        b_z(zs, side, part).start()
-                elif part == side:
-                    b_z(zs, side, part).wait_recv()
+    def take_b(d, part):
+        for side in range(2):
+            zs = zfrom(side, d)
+            if d < 4:
+                b_z(zs, side, part).wait_recv()
+                if d < 3 or part == side:
+                    b_z(zs, side, part).start()
+            elif part == side:
+                b_z(zs, side, part).wait_recv()
 
     def hop(d):
         for side in range(2 if 0 < d < 4 else 1):
@@ -180,17 +179,33 @@
         for part in range(2):
             for side in range(2):
                 b_z(z, side, part).start()
+        take_a(2)
         hop(0)
-        take_a(2)
         early()
-        for d in range(5):
-            if d < 4:
-                hop(d + 1)
-                take_b(d + 1)
-            end(d)
-            compute(d)
-            if d < 2:
-                take_a(d + 3)
+        take_b(1, 0)
+        take_b(1, 1)
+        hop(1)
+        hop(2)
+        take_a(3)
+        take_b(2, 0)
+        take_b(2, 1)
+        take_a(4)
+        take_b(3, 0)
+        end(1)
+        hop(3)
+        end(0)
+        end(2)
+        compute(2)
+        take_b(3, 1)
+        hop(4)
+        compute(0)
+        compute(1)
+        end(3)
+        compute(3)
+        take_b(4, 0)
+        take_b(4, 1)
+        end(4)
+        compute(4)
 
     def gather_drain():
         for i in range(1, NX):
@@ -218,7 +233,6 @@
     def early():
         for i in range(2, 5):
             loads[i].wait()
-        acc[...] = jnp.zeros_like(acc)
         c0 = cv[...]
         CQ[0:KL, :] = c0.astype(BF16)
         NB[...] = jnp.broadcast_to(jnp.sum(c0 * c0, axis=1, keepdims=True), (KL, 128))
@@ -243,17 +257,6 @@
             st_s.at[zc, xc], st_r.at[it, zs, xs], st_ss.at[zc, xc], st_rs.at[it, zs, xs], cdev(xc, zc)
         )
 
-    def logit_part(zc, dots, lo, n, h):
-        nb = NB[lo:lo + n, :]
-        for xc in range(NX):
-            a = xc * BLOCK
-            ll = sharpness * (2.0 * dots[0:n, a:a + BLOCK] - nb)
-            m = jnp.max(ll, axis=0, keepdims=True)
-            e = jnp.exp(ll - m)
-            E[zc, lo:lo + n, a:a + BLOCK] = e
-            ml[zc, h:h + 1, a:a + BLOCK] = m
-            sl[zc, h:h + 1, a:a + BLOCK] = jnp.sum(e, axis=0, keepdims=True)
-
     def dot_nt(lhs, rhs):
         return lax.dot_general(lhs, rhs, (((1,), (1,)), ((), ())), preferred_element_type=F32)
 
@@ -266,77 +269,43 @@
             for xc in range(NX):
                 st_copy(it, xc, zc, x, z).start()
 
-    def first_column(zc, mine):
-        dots = dot_nt(CQ[...], G[zc].reshape(NX * BLOCK, D))
-        logit_part(zc, dots, 0, KL, 0)
-        S[zc] = dots[KL:KL + QP, :] * sharpness
-        m = ml[zc, 0:1, :]
-        s = sl[zc, 0:1, :]
-        ml[zc, 1:2, :] = m
-        for xc in range(NX):
-            st_s[zc, xc, 0:1, :] = m[:, xc * BLOCK:(xc + 1) * BLOCK]
-            st_s[zc, xc, 1:2, :] = s[:, xc * BLOCK:(xc + 1) * BLOCK]
-        ship(0, zc, mine)
+    def columns(it, zcs):
+        for zc in zcs:
+            lhs = CQ[...] if it == 0 else C2[:, 0:D]
+            dots = dot_nt(lhs, G[zc].reshape(NX * BLOCK, D))
+            nb = NB[...]
+            for xc in range(NX):
+                a = xc * BLOCK
+                ll = sharpness * (2.0 * dots[0:KL, a:a + BLOCK] - nb)
+                m = jnp.max(ll, axis=0, keepdims=True)
+                e = jnp.exp(ll - m)
+                E[zc, :, a:a + BLOCK] = e
+                st_s[zc, xc, 0:1, :] = m
+                st_s[zc, xc, 1:2, :] = jnp.sum(e, axis=0, keepdims=True)
+            if it == 0:
+                S[zc] = dots[KL:KL + QP, :] * sharpness
 
     def softmax_first():
         def compute(d):
-            if d == 0:
-                first_column(z, True)
-            elif d == 4:
-                first_column(zfrom(0, 4), False)
-            else:
-                def side_step(i, _):
-                    first_column((z + NZ + (2 * i - 1) * d) % NZ, False)
-                    return 0
-
-                lax.fori_loop(0, 2, side_step, 0)
+            zcs = [zfrom(side, d) for side in range(2 if 0 < d < 4 else 1)]
+            columns(0, zcs)
+            for zc in zcs:
+                ship(0, zc, d == 0)
 
         gather(compute)
-
-    def second_column(zc, h):
-        dots = dot_nt(C2[h * RC:(h + 1) * RC, 0:D], G[zc].reshape(NX * BLOCK, D))
-        logit_part(zc, dots, h * RC, RC, h)
-
-    def second_ship(zc, mine):
-        for xc in range(NX):
-            a = xc * BLOCK
-            ma, mb = ml[zc, 0:1, a:a + BLOCK], ml[zc, 1:2, a:a + BLOCK]
-            m = jnp.maximum(ma, mb)
-            st_s[zc, xc, 0:1, :] = m
-            st_s[zc, xc, 1:2, :] = (
-                sl[zc, 0:1, a:a + BLOCK] * jnp.exp(ma - m) + sl[zc, 1:2, a:a + BLOCK] * jnp.exp(mb - m)
-            )
-        ship(1, zc, mine)
 
     def softmax_second():
         for h in range(CH):
             rows_wait(0, h)
-            rows = slice(h * RC, (h + 1) * RC)
-            NB[rows, :] = jnp.broadcast_to(
-                jnp.sum(C2[rows, D:W].astype(F32), axis=1, keepdims=True), (RC, 128)
-            )
-            if h < CH - 1:
-                def part(zc, _):
-                    second_column(zc, h)
-                    return 0
-
-                lax.fori_loop(0, NZ, part, 0)
-            else:
-                def last(k, _):
-                    zc = column(k)
-                    second_column(zc, h)
-                    second_ship(zc, False)
-                    return 0
-
-                second_column(z, h)
-                second_ship(z, True)
-                lax.fori_loop(1, NZ, last, 0)
+        NB[...] = jnp.broadcast_to(jnp.sum(C2[:, D:W].astype(F32), axis=1, keepdims=True), (KL, 128))
+        for grp in ((7, 6, 5, 4), (3, 2, 1, 0)):
+            columns(1, [column(k) for k in grp])
+            for k in grp:
+                ship(1, column(k), k == 0)
 
     def rs_copy(it, o, xo, zo):
-        peer = (me + o) % CENT
-        return rcopy(
-            rs_r.at[it, z, x], rs_r.at[it, zo, xo], rs_ss.at[it, o], rs_rs.at[it, zo, xo], (dp, peer)
-        )
+        dev = cdev((x + o // NZ) % NX, (z + o % NZ) % NZ)
+        return rcopy(rs_r.at[it, z, x], rs_r.at[it, zo, xo], rs_ss.at[it, o], rs_rs.at[it, zo, xo], dev)
 
     def owner_combine(it):
         def w(o, _):
@@ -352,11 +321,10 @@
         rs_r[it, z, x, 0:1, :] = top
         rs_r[it, z, x, 1:2, :] = 1.0 / tot
 
-        def snd(o, _):
-            rs_copy(it, o, x, z).start()
-            return 0
-
-        lax.fori_loop(1, CENT, snd, 0)
+        for dz in (4, 3, 5, 2, 6, 1, 7, 0):
+            for dx in (2, 1, 3, 0):
+                if dz or dx:
+                    rs_copy(it, dx * NZ + dz, x, z).start()
 
     def query_post():
         pats = [patb[i] for i in range(4)]
@@ -444,24 +412,23 @@
 
         lax.fori_loop(1, CENT, ws, 0)
 
-    def numer(it, h, lo, hi):
+    def numer(it, h):
         rows = slice(h * RC, (h + 1) * RC)
-
-        def col(zc, _):
-            cnt = acc[it, rows, D:W]
+        cnt = jnp.zeros((RC, BLOCK), F32)
+        tot = jnp.zeros((RC, D), F32)
+        for zc in range(NZ):
             parts = []
             for xc in range(NX):
                 a = xc * BLOCK
-                g = jnp.exp(ml[zc, h:h + 1, a:a + BLOCK] - rs_r[it, zc, xc, 0:1, :]) * rs_r[it, zc, xc, 1:2, :]
+                g = jnp.exp(st_s[zc, xc, 0:1, :] - rs_r[it, zc, xc, 0:1, :]) * rs_r[it, zc, xc, 1:2, :]
                 r = E[zc, rows, a:a + BLOCK] * g
                 cnt = cnt + r
                 parts.append(r.astype(BF16))
-            acc[it, rows, D:W] = cnt
-            r_all = jnp.concatenate(parts, axis=1)
-            acc[it, rows, 0:D] += jnp.dot(r_all, G[zc].reshape(NX * BLOCK, D), preferred_element_type=F32)
-            return 0
-
-        lax.fori_loop(lo, hi, col, 0)
+            tot = tot + jnp.dot(
+                jnp.concatenate(parts, axis=1), G[zc].reshape(NX * BLOCK, D), preferred_element_type=F32
+            )
+        acc[it, rows, 0:D] = tot
+        acc[it, rows, D:W] = cnt
 
     mine_at = [pl.multiple_of(h * RC + core * RH, RH) for h in range(CH)]
     theirs_at = [pl.multiple_of(h * RC + RH - core * RH, RH) for h in range(CH)]
@@ -530,26 +497,28 @@
             half_copy(it, h).wait_send()
 
     def finish():
-        if STOP >= 0:
-            gather_drain()
-
-        def wsq(o, _):
-            q_copy(o, dp).wait_send()
-            return 0
-
-        lax.fori_loop(1, DP, wsq, 0)
+        if STOP < 1:
+            early_drain()
         if STOP < 90:
             out_ref[...] = jnp.zeros_like(out_ref)
             loss_ref[...] = jnp.zeros_like(loss_ref)
 
+    def early_drain():
+        if STOP >= 0:
+            gather_drain()
+
+        def wsq(o, _):
+            q_copy(o, dp).wait_send()
+            return 0
+
+        lax.fori_loop(1, DP, wsq, 0)
+
     def mid(it):
-        numer(it, 0, 0, NZ)
-        pair_copy(it, 0).start()
-        numer(it, 1, 0, NZ // 2)
-        pair_sum(it, 0)
-        numer(it, 1, NZ // 2, NZ)
-        pair_copy(it, 1).start()
-        pair_sum(it, 1)
+        for h in range(CH):
+            numer(it, h)
+            pair_copy(it, h).start()
+        for h in range(CH):
+            pair_sum(it, h)
 
     if STOP == -2:
         for o in range(1, DP):
@@ -568,6 +537,7 @@
         return finish()
     softmax_first()
     owner_combine(0)
+    early_drain()
     if STOP == 1:
         stats_wait(0)
         stats_drain(0)
@@ -644,8 +614,6 @@
             pltpu.VMEM((4, 1024), jnp.int32),
             pltpu.VMEM((DP, 128), jnp.int32),
             pltpu.VMEM((5, QP, 128), F32),
-            pltpu.VMEM((NZ, CH, NX * BLOCK), F32),
-            pltpu.VMEM((NZ, CH, NX * BLOCK), F32),
             pltpu.VMEM((NZ, NX, 2, 128), F32),
             pltpu.VMEM((2, NZ, NX, 2, 128), F32),
             pltpu.VMEM((2, NZ, NX, 2, 128), F32),

time: 120 us -> 110 us (0.917)
  Pallas kernels: 117 us -> 106 us
    pallas_call x1, Pallas kernels: 117 us -> 106 us  [on_device(): pl.pallas_call(kernel, out_shape=(jax.ShapeDtypeStruct((KL, D), BF16), ja...]
where the time goes in v4:
time: 110 us
  Pallas kernels  106 us (96%)
  other arithmetic  1.93 us (2%)
    pallas_call x1, Pallas kernels, on_device(): pl.pallas_call(kernel, out_shape=(jax.ShapeDtypeStruct((KL, D), BF16), ja...  106 us

profile of v4, /device:TPU:1, one launch (start us, length us, event | category | flops | bytes accessed | tf_op | source)
XLA Modules:
  0.0 109.6 jit_solution(2221651114829120113)
XLA Ops:
  0.6 106.5 %shard_map.68 = (bf16[256,768]{1,0:T(8,128)(2,1)}, f32[1,4]{1,0:T(1,128)}) custom-call(bf16[128,768]{1,0:T(8,128)(2,1)} %p_ref.1, bf16[4,768]{1,0:T(4,128)(2,1)} %q_ref.1, f32[256,768]{1,0:T(8,128)} %c_ref.1, s32[4,1024]{1,0:T(4,128)} %bitcast.3, s32[8,128]{1,0:T(8,128)} %bitcast.4), custom_call_target="tpu_custom_call" | custom-call | tf_op jit(solution)/shard_map/pallas_call | solution.py:594
  107.1 0.0 copy-start
  107.1 1.9 %convert_element_type.3 = f32[256,768]{1,0:T(8,128)} convert(bf16[256,768]{1,0:T(8,128)(2,1)} %get-tuple-element.4) | non-fusion elementwise | flops 196608 | bytes 1179648 | tf_op jit(solution)/shard_map/convert_element_type | solution.py:639
  109.1 0.0 copy-done
  109.1 0.5 copy.8
Async XLA Ops:
  107.1 1.9 %copy-start = (f32[1,4]{1,0:T(1,128)S(1)}, f32[1,4]{1,0:T(1,128)}, u32[]{:S(2)}) copy-start(f32[1,4]{1,0:T(1,128)} %get-tuple-element.5) | copy-start | bytes 52

commit v5 on v4

--- a/solution.py
+++ b/solution.py
@@ -25,6 +25,7 @@
 RA = 80
 RB = 128 - RA
 NARROW = (True, False)
+FAR, NEAR = (0, 1, 2, 3), (4, 5, 6, 7)
 F32 = jnp.float32
 BF16 = jnp.bfloat16
 
@@ -56,6 +57,7 @@
     x, z = me // NZ, me % NZ
     y, core = dp // 2, dp % 2
     sib = (dp + 1 - 2 * core, me)
+    z4 = (z + NZ // 2) % NZ
 
     def cdev(xx, zz):
         return (dp, xx * NZ + zz)
@@ -194,12 +196,12 @@
         end(1)
         hop(3)
         end(0)
+        compute(0)
         end(2)
-        compute(2)
+        compute(1)
         take_b(3, 1)
         hop(4)
-        compute(0)
-        compute(1)
+        compute(2)
         end(3)
         compute(3)
         take_b(4, 0)
@@ -254,7 +256,8 @@
 
     def st_copy(it, xc, zc, xs, zs):
         return rcopy(
-            st_s.at[zc, xc], st_r.at[it, zs, xs], st_ss.at[zc, xc], st_rs.at[it, zs, xs], cdev(xc, zc)
+            st_s.at[zc * NX + xc], st_r.at[it, zs * NX + xs], st_ss.at[it], st_rs.at[it],
+            cdev(xc, (zc + NZ // 2) % NZ),
         )
 
     def dot_nt(lhs, rhs):
@@ -262,9 +265,9 @@
 
     def ship(it, zc, mine):
         if mine:
-            st_r[it, z, x] = st_s[z, x]
+            st_r[it, z * NX + x] = st_s[z4 * NX + x]
             for i in range(1, NX):
-                st_copy(it, (x + i) % NX, z, x, z).start()
+                st_copy(it, (x + i) % NX, z4, x, z).start()
         else:
             for xc in range(NX):
                 st_copy(it, xc, zc, x, z).start()
@@ -280,8 +283,8 @@
                 m = jnp.max(ll, axis=0, keepdims=True)
                 e = jnp.exp(ll - m)
                 E[zc, :, a:a + BLOCK] = e
-                st_s[zc, xc, 0:1, :] = m
-                st_s[zc, xc, 1:2, :] = jnp.sum(e, axis=0, keepdims=True)
+                st_s[zc * NX + xc, 0:1, :] = m
+                st_s[zc * NX + xc, 1:2, :] = jnp.sum(e, axis=0, keepdims=True)
             if it == 0:
                 S[zc] = dots[KL:KL + QP, :] * sharpness
 
@@ -290,7 +293,7 @@
             zcs = [zfrom(side, d) for side in range(2 if 0 < d < 4 else 1)]
             columns(0, zcs)
             for zc in zcs:
-                ship(0, zc, d == 0)
+                ship(0, zc, d == 4)
 
         gather(compute)
 
@@ -298,33 +301,32 @@
         for h in range(CH):
             rows_wait(0, h)
         NB[...] = jnp.broadcast_to(jnp.sum(C2[:, D:W].astype(F32), axis=1, keepdims=True), (KL, 128))
-        for grp in ((7, 6, 5, 4), (3, 2, 1, 0)):
+        for grp in (FAR, NEAR):
             columns(1, [column(k) for k in grp])
             for k in grp:
-                ship(1, column(k), k == 0)
-
-    def rs_copy(it, o, xo, zo):
-        dev = cdev((x + o // NZ) % NX, (z + o % NZ) % NZ)
-        return rcopy(rs_r.at[it, z, x], rs_r.at[it, zo, xo], rs_ss.at[it, o], rs_rs.at[it, zo, xo], dev)
+                ship(1, column(k), k == 7)
+
+    def rs_copy(it, dx, dz):
+        ref = rs_r.at[it, z4 * NX + x]
+        far = 1 if dz in (3, 4, 5, 6) else 0
+        return rcopy(ref, ref, rs_ss.at[it], rs_rs.at[it, far], cdev((x + dx) % NX, (z + dz) % NZ))
+
+    def all_of(ref, n, ss, rs):
+        some = ref.at[pl.ds(0, n)]
+        return rcopy(some, some, ss, rs, sib)
 
     def owner_combine(it):
-        def w(o, _):
-            src = (me + o) % CENT
-            st_copy(it, x, z, src // NZ, src % NZ).wait_recv()
-            return 0
-
-        lax.fori_loop(1, CENT, w, 0)
-        m = st_r[it, :, :, 0:1, :].reshape(CENT, 1, BLOCK)
-        s = st_r[it, :, :, 1:2, :].reshape(CENT, 1, BLOCK)
+        all_of(st_r.at[it], CENT - 1, st_ss.at[it], st_rs.at[it]).wait_recv()
+        m = st_r[it, :, 0:1, :]
+        s = st_r[it, :, 1:2, :]
         top = jnp.max(m, axis=0)
         tot = jnp.sum(s * jnp.exp(m - top[None]), axis=0)
-        rs_r[it, z, x, 0:1, :] = top
-        rs_r[it, z, x, 1:2, :] = 1.0 / tot
-
-        for dz in (4, 3, 5, 2, 6, 1, 7, 0):
+        rs_r[it, z4 * NX + x, 0:1, :] = top
+        rs_r[it, z4 * NX + x, 1:2, :] = 1.0 / tot
+        for dz in (4, 3, 5, 6, 2, 1, 7, 0):
             for dx in (2, 1, 3, 0):
                 if dz or dx:
-                    rs_copy(it, dx * NZ + dz, x, z).start()
+                    rs_copy(it, dx, dz).start()
 
     def query_post():
         pats = [patb[i] for i in range(4)]
@@ -395,46 +397,42 @@
 
         lax.fori_loop(1, DP, ws, 0)
 
-    def stats_wait(it):
-        def w(o, _):
-            src = (me + o) % CENT
-            rs_copy(it, o, src // NZ, src % NZ).wait_recv()
-            return 0
-
-        lax.fori_loop(1, CENT, w, 0)
+    def stats_wait(it, grp):
+        n, far = (16, 1) if grp is FAR else (15, 0)
+        all_of(rs_r.at[it], n, rs_ss.at[it], rs_rs.at[it, far]).wait_recv()
 
     def stats_drain(it):
-        def ws(o, _):
-            dst = (me + o) % CENT
-            st_copy(it, dst // NZ, dst % NZ, x, z).wait_send()
-            rs_copy(it, o, x, z).wait_send()
-            return 0
-
-        lax.fori_loop(1, CENT, ws, 0)
-
-    def numer(it, h):
-        rows = slice(h * RC, (h + 1) * RC)
+        all_of(st_r.at[it], CENT - 1, st_ss.at[it], st_rs.at[it]).wait_send()
+        all_of(rs_r.at[it], CENT - 1, rs_ss.at[it], rs_rs.at[it, 0]).wait_send()
+
+    def numer(it, h, grp):
+        rows = pl.ds(pl.multiple_of(h * RC, RC), RC)
         cnt = jnp.zeros((RC, BLOCK), F32)
         tot = jnp.zeros((RC, D), F32)
-        for zc in range(NZ):
+        for k in grp:
+            zc = column(k)
             parts = []
             for xc in range(NX):
                 a = xc * BLOCK
-                g = jnp.exp(st_s[zc, xc, 0:1, :] - rs_r[it, zc, xc, 0:1, :]) * rs_r[it, zc, xc, 1:2, :]
+                g = jnp.exp(st_s[zc * NX + xc, 0:1, :] - rs_r[it, zc * NX + xc, 0:1, :]) * rs_r[it, zc * NX + xc, 1:2, :]
                 r = E[zc, rows, a:a + BLOCK] * g
                 cnt = cnt + r
                 parts.append(r.astype(BF16))
             tot = tot + jnp.dot(
                 jnp.concatenate(parts, axis=1), G[zc].reshape(NX * BLOCK, D), preferred_element_type=F32
             )
-        acc[it, rows, 0:D] = tot
-        acc[it, rows, D:W] = cnt
+        if grp is NEAR:
+            acc[it, rows, 0:D] = tot
+            acc[it, rows, D:W] = cnt
+        else:
+            acc[it, rows, 0:D] += tot
+            acc[it, rows, D:W] += cnt
 
     mine_at = [pl.multiple_of(h * RC + core * RH, RH) for h in range(CH)]
     theirs_at = [pl.multiple_of(h * RC + RH - core * RH, RH) for h in range(CH)]
 
     def pair_copy(it, h):
-        return rcopy(acc.at[it, pl.ds(theirs_at[h], RH)], rb1.at[it, h], n1_ss.at[it, h], n1_rs.at[it, h], sib)
+        return rcopy(acc.at[it, pl.ds(pl.multiple_of(h * RC + RH - core * RH, RH), RH)], rb1.at[it, h], n1_ss.at[it, h], n1_rs.at[it, h], sib)
 
     def quarter(h, yy):
         return pl.ds(pl.multiple_of(h * RC + core * RH + yy * RQ, RQ), RQ)
@@ -514,9 +512,19 @@
         lax.fori_loop(1, DP, wsq, 0)
 
     def mid(it):
-        for h in range(CH):
-            numer(it, h)
+        stats_wait(it, NEAR)
+        def near(h, _):
+            numer(it, h, NEAR)
+            return 0
+
+        lax.fori_loop(0, CH, near, 0)
+        stats_wait(it, FAR)
+        def far(h, _):
+            numer(it, h, FAR)
             pair_copy(it, h).start()
+            return 0
+
+        lax.fori_loop(0, CH, far, 0)
         for h in range(CH):
             pair_sum(it, h)
 
@@ -539,12 +547,14 @@
     owner_combine(0)
     early_drain()
     if STOP == 1:
-        stats_wait(0)
+        stats_wait(0, NEAR)
+        stats_wait(0, FAR)
         stats_drain(0)
         return finish()
     query_post()
-    stats_wait(0)
     if STOP == 2:
+        stats_wait(0, NEAR)
+        stats_wait(0, FAR)
         stats_drain(0)
         query_finish()
         return finish()
@@ -568,8 +578,9 @@
     softmax_second()
     owner_combine(1)
     query_finish()
-    stats_wait(1)
     if STOP == 6:
+        stats_wait(1, NEAR)
+        stats_wait(1, FAR)
         stats_drain(1)
         reduce_drain(0)
         return finish()
@@ -614,9 +625,9 @@
             pltpu.VMEM((4, 1024), jnp.int32),
             pltpu.VMEM((DP, 128), jnp.int32),
             pltpu.VMEM((5, QP, 128), F32),
-            pltpu.VMEM((NZ, NX, 2, 128), F32),
-            pltpu.VMEM((2, NZ, NX, 2, 128), F32),
-            pltpu.VMEM((2, NZ, NX, 2, 128), F32),
+            pltpu.VMEM((CENT, 2, 128), F32),
+            pltpu.VMEM((2, CENT, 2, 128), F32),
+            pltpu.VMEM((2, CENT, 2, 128), F32),
             pltpu.VMEM((8, D), F32),
             pltpu.VMEM((DP, 8, D), F32),
             pltpu.VMEM((DP, 8, 128), F32),
@@ -624,8 +635,8 @@
             dma((NZ, 2)), dma((NZ + 1,)), dma((NZ, 2, 2)), dma((NZ, 2)),
             dma((NZ, 4)), dma((NZ, 4)), dma((4,)), dma((4,)),
             dma((DP,)), dma((DP,)),
-            dma((NZ, NX)), dma((2, NZ, NX)),
-            dma((2, CENT)), dma((2, NZ, NX)),
+            dma((2,)), dma((2,)),
+            dma((2,)), dma((2, 2)),
             dma((2, CH)), dma((2, CH)),
             dma((2, CH, NY)), dma((2, CH, NY)),
             dma((2, CH, NY)), dma((2, CH, NY)),

time: 110 us -> 103 us (0.936)
  Pallas kernels: 106 us -> 99.9 us
    pallas_call x1, Pallas kernels: 106 us -> 99.9 us  [on_device(): pl.pallas_call(kernel, out_shape=(jax.ShapeDtypeStruct((KL, D), BF16), ja...]
where the time goes in v5:
time: 103 us
  Pallas kernels  99.9 us (97%)
  other arithmetic  1.93 us (2%)
    pallas_call x1, Pallas kernels, on_device(): pl.pallas_call(kernel, out_shape=(jax.ShapeDtypeStruct((KL, D), BF16), ja...  99.9 us

profile of v5, /device:TPU:1, one launch (start us, length us, event | category | flops | bytes accessed | tf_op | source)
XLA Modules:
  0.0 103.0 jit_solution(1210273674237597764)
XLA Ops:
  0.6 99.9 %shard_map.68 = (bf16[256,768]{1,0:T(8,128)(2,1)}, f32[1,4]{1,0:T(1,128)}) custom-call(bf16[128,768]{1,0:T(8,128)(2,1)} %p_ref.1, bf16[4,768]{1,0:T(4,128)(2,1)} %q_ref.1, f32[256,768]{1,0:T(8,128)} %c_ref.1, s32[4,1024]{1,0:T(4,128)} %bitcast.3, s32[8,128]{1,0:T(8,128)} %bitcast.4), custom_call_target="tpu_custom_call" | custom-call | tf_op jit(solution)/shard_map/pallas_call | solution.py:605
  100.5 0.0 copy-start
  100.5 1.9 %convert_element_type.3 = f32[256,768]{1,0:T(8,128)} convert(bf16[256,768]{1,0:T(8,128)(2,1)} %get-tuple-element.4) | non-fusion elementwise | flops 196608 | bytes 1179648 | tf_op jit(solution)/shard_map/convert_element_type | solution.py:650
  102.5 0.0 copy-done
  102.5 0.5 copy.8
Async XLA Ops:
  100.5 1.9 %copy-start = (f32[1,4]{1,0:T(1,128)S(1)}, f32[1,4]{1,0:T(1,128)}, u32[]{:S(2)}) copy-start(f32[1,4]{1,0:T(1,128)} %get-tuple-element.5) | copy-start | bytes 52

commit v6 on v5

--- a/solution.py
+++ b/solution.py
@@ -24,7 +24,7 @@
 STOP = 99
 RA = 80
 RB = 128 - RA
-NARROW = (True, False)
+NARROW = (True, True)
 FAR, NEAR = (0, 1, 2, 3), (4, 5, 6, 7)
 F32 = jnp.float32
 BF16 = jnp.bfloat16
@@ -100,19 +100,19 @@
     def a_z(zs, side, part=None):
         lo, n = (0, D) if part is None else (part * HD, HD)
         ref = G.at[zs, x, pl.ds(0, RA), pl.ds(lo, n)]
-        return rcopy(ref, ref, az_ss.at[zs, side], az_rs.at[zs if part != 1 else NZ], zdev(STEP[side]))
+        return rcopy(ref, ref, az_ss, az_rs.at[zs if part != 1 else NZ], zdev(STEP[side]))
 
     def b_z(zs, side, part):
         ref = G.at[zs, pl.ds(part * (NX // 2), NX // 2), pl.ds(RA, RB)]
-        return rcopy(ref, ref, bz_ss.at[zs, side, part], bz_rs.at[zs, part], zdev(STEP[side]))
+        return rcopy(ref, ref, bz_ss, bz_rs.at[zs, part], zdev(STEP[side]))
 
     def a_x(zs, xs, side):
         ref = G.at[zs, xs, pl.ds(0, RA)]
-        return rcopy(ref, ref, ax_ss.at[zs, side], ax_rs.at[zs, side], xdev(STEP[side]))
+        return rcopy(ref, ref, ax_ss.at[0], ax_rs.at[zs, side], xdev(STEP[side]))
 
     def a_x2(zs, xs, side):
         ref = G.at[zs, xs, pl.ds(0, RA), pl.ds(side * HD, HD)]
-        return rcopy(ref, ref, ax_ss.at[zs, 2 + side], ax_rs.at[zs, 2 + side], xdev(STEP[side]))
+        return rcopy(ref, ref, ax_ss.at[1], ax_rs.at[zs, 2 + side], xdev(STEP[side]))
 
     def b_x(xs, i):
         ref = G.at[z, xs, pl.ds(RA, RB)]
@@ -212,21 +212,16 @@
     def gather_drain():
         for i in range(1, NX):
             b_x(x, i).wait_send()
-        for side in range(2):
-            for d in range(4):
-                zs = zfrom(side, d)
-                a_z(zs, side, None if d < 3 else side).wait_send()
-                for part in range(2):
-                    if d < 3 or part == side:
-                        b_z(zs, side, part).wait_send()
-
-        def w(zs, _):
-            for side in range(2):
-                a_x(zs, x, side).wait_send()
-                a_x2(zs, xfrom(side), side).wait_send()
-            return 0
-
-        lax.fori_loop(0, NZ, w, 0)
+
+        def wait_all(ref, ss):
+            rcopy(ref, ref, ss, bx_rs.at[0], sib).wait_send()
+
+        flat = G.at[:, :, pl.ds(0, RA)]
+        wait_all(flat.at[0, pl.ds(0, 1)], az_ss)
+        wait_all(flat.at[pl.ds(0, 3), pl.ds(0, 2)], az_ss)
+        wait_all(G.at[pl.ds(0, 7), :, pl.ds(RA, RB)], bz_ss)
+        wait_all(flat.at[pl.ds(0, 4)], ax_ss.at[0])
+        wait_all(flat.at[pl.ds(0, 2)], ax_ss.at[1])
 
     def q_wait(o, _):
         q_copy(o, (dp + DP - o) % DP).wait_recv()
@@ -246,7 +241,8 @@
                 row = patv[i:i + 1, j * BLOCK:(j + 1) * BLOCK] if i < 4 else offv[j:j + 1, :]
                 vals = jnp.where(pick, jnp.broadcast_to(row.astype(F32), (8, BLOCK)), 0.0)
                 patb[i, 8 * j:8 * j + 8, :] = jnp.broadcast_to(jnp.sum(vals, axis=1, keepdims=True), (8, BLOCK))
-        lax.fori_loop(1, DP, q_wait, 0)
+        for o in range(1, DP):
+            q_wait(o, 0)
         CQ[KL:KL + QP, :] = qr[...].reshape(QP, D).astype(BF16)
 
     def column(k):
@@ -632,8 +628,8 @@
             pltpu.VMEM((DP, 8, D), F32),
             pltpu.VMEM((DP, 8, 128), F32),
             pltpu.VMEM((DP, 8, 128), F32),
-            dma((NZ, 2)), dma((NZ + 1,)), dma((NZ, 2, 2)), dma((NZ, 2)),
-            dma((NZ, 4)), dma((NZ, 4)), dma((4,)), dma((4,)),
+            dma, dma((NZ + 1,)), dma, dma((NZ, 2)),
+            dma((2,)), dma((NZ, 4)), dma((4,)), dma((4,)),
             dma((DP,)), dma((DP,)),
             dma((2,)), dma((2,)),
             dma((2,)), dma((2, 2)),

time: 103 us -> 100 us (0.971)
  Pallas kernels: 99.9 us -> 97 us
    pallas_call x1, Pallas kernels: 99.9 us -> 97 us  [on_device(): pl.pallas_call(kernel, out_shape=(jax.ShapeDtypeStruct((KL, D), BF16), ja...]
where the time goes in v6:
time: 100 us
  Pallas kernels  97 us (97%)
  other arithmetic  1.93 us (2%)
    pallas_call x1, Pallas kernels, on_device(): pl.pallas_call(kernel, out_shape=(jax.ShapeDtypeStruct((KL, D), BF16), ja...  97 us

profile of v6, /device:TPU:1, one launch (start us, length us, event | category | flops | bytes accessed | tf_op | source)
XLA Modules:
  0.0 100.1 jit_solution(13322741250060220727)
XLA Ops:
  0.6 97.0 %shard_map.68 = (bf16[256,768]{1,0:T(8,128)(2,1)}, f32[1,4]{1,0:T(1,128)}) custom-call(bf16[128,768]{1,0:T(8,128)(2,1)} %p_ref.1, bf16[4,768]{1,0:T(4,128)(2,1)} %q_ref.1, f32[256,768]{1,0:T(8,128)} %c_ref.1, s32[4,1024]{1,0:T(4,128)} %bitcast.3, s32[8,128]{1,0:T(8,128)} %bitcast.4), custom_call_target="tpu_custom_call" | custom-call | tf_op jit(solution)/shard_map/pallas_call | solution.py:601
  97.6 0.0 copy-start
  97.6 1.9 %convert_element_type.3 = f32[256,768]{1,0:T(8,128)} convert(bf16[256,768]{1,0:T(8,128)(2,1)} %get-tuple-element.4) | non-fusion elementwise | flops 196608 | bytes 1179648 | tf_op jit(solution)/shard_map/convert_element_type | solution.py:646
  99.5 0.0 copy-done
  99.6 0.5 copy.8
Async XLA Ops:
  97.6 1.9 %copy-start = (f32[1,4]{1,0:T(1,128)S(1)}, f32[1,4]{1,0:T(1,128)}, u32[]{:S(2)}) copy-start(f32[1,4]{1,0:T(1,128)} %get-tuple-element.5) | copy-start | bytes 52

commit v7 on v6

--- a/solution.py
+++ b/solution.py
@@ -21,10 +21,8 @@
 RQ = RH // NY
 sharpness = 0.05
 NEG = -1e30
-STOP = 99
 RA = 80
 RB = 128 - RA
-NARROW = (True, True)
 FAR, NEAR = (0, 1, 2, 3), (4, 5, 6, 7)
 F32 = jnp.float32
 BF16 = jnp.bfloat16
@@ -47,7 +45,7 @@
 
 def kernel(
     p_ref, q_ref, c_ref, pat_ref, off_ref, out_ref, loss_ref,
-    G, E, S, CQ, C2, NB, acc, rb1, nar, rb2n, rb2, own, cv, qv, patv, offv, patb, st_s, st_r, rs_r,
+    G, E, S, CQ, C2, NB, acc, rb1, nar, rb2n, own, cv, qv, patv, offv, patb, st_s, st_r, rs_r,
     qs, qr, qp_s, qp_r,
     az_ss, az_rs, bz_ss, bz_rs, ax_ss, ax_rs, bx_ss, bx_rs, q_ss, q_rs, st_ss, st_rs, rs_ss, rs_rs,
     n1_ss, n1_rs, n2_ss, n2_rs, c_ss, c_rs, qp_ss, qp_rs, loc,
@@ -296,7 +294,10 @@
     def softmax_second():
         for h in range(CH):
             rows_wait(0, h)
-        NB[...] = jnp.broadcast_to(jnp.sum(C2[:, D:W].astype(F32), axis=1, keepdims=True), (KL, 128))
+            rows = slice(h * RC, (h + 1) * RC)
+            NB[rows, :] = jnp.broadcast_to(
+                jnp.sum(C2[rows, D:W].astype(F32), axis=1, keepdims=True), (RC, 128)
+            )
         for grp in (FAR, NEAR):
             columns(1, [column(k) for k in grp])
             for k in grp:
@@ -435,27 +436,25 @@
 
     def y_copy(it, h, i):
         yp = (y + i) % NY
-        sem = (n2_ss.at[it, h, i], n2_rs.at[it, h, i])
-        if NARROW[it]:
-            src = nar.at[it, h, pl.ds(pl.multiple_of(yp * RQ, RQ), RQ)]
-            return rcopy(src, rb2n.at[it, h, i], *sem, (yp * 2 + core, me))
-        return rcopy(acc.at[it, quarter(h, yp)], rb2.at[it, h, i], *sem, (yp * 2 + core, me))
+        sem = (n2_ss.at[it, h], n2_rs.at[it, h])
+        src = nar.at[it, h, pl.ds(pl.multiple_of(yp * RQ, RQ), RQ)]
+        return rcopy(src, rb2n.at[it, h, i], *sem, (yp * 2 + core, me))
 
     def pair_sum(it, h):
         pair_copy(it, h).wait_recv()
         tot = acc[it, pl.ds(mine_at[h], RH), :] + rb1[it, h]
         acc[it, pl.ds(mine_at[h], RH), :] = tot
-        if NARROW[it]:
-            nar[it, h, :, 0:D] = tot[:, 0:D].astype(BF16)
-            nar[it, h, :, D:W] = three(jnp.sum(tot[:, D:W], axis=1, keepdims=True), RH)
+        nar[it, h, :, 0:D] = tot[:, 0:D].astype(BF16)
+        nar[it, h, :, D:W] = three(jnp.sum(tot[:, D:W], axis=1, keepdims=True), RH)
         for i in (2, 1, 3):
             y_copy(it, h, i).start()
 
     def update(it, h):
         tot = acc[it, quarter(h, y), :]
-        for i in (1, 3, 2):
-            y_copy(it, h, i).wait_recv()
-            tot = tot + (rb2n[it, h, i].astype(F32) if NARROW[it] else rb2[it, h, i])
+        got = rb2n.at[it, h, pl.ds(1, NY - 1)]
+        rcopy(got, got, n2_ss.at[it, h], n2_rs.at[it, h], sib).wait_recv()
+        for i in (1, 2, 3):
+            tot = tot + rb2n[it, h, i].astype(F32)
         counts = jnp.sum(tot[:, D:W], axis=1, keepdims=True)
         cold = cv[quarter(h, y), :] if it == 0 else own[h]
         return (tot[:, 0:D] + cold) / (counts + 1.0)
@@ -463,7 +462,7 @@
     def row_copy(k, h, i):
         arr = C2 if k == 0 else out_ref
         ref = arr.at[quarter(h, y)]
-        return rcopy(ref, ref, c_ss.at[k, h, i], c_rs.at[k, h, i], (((y + i) % NY) * 2 + core, me))
+        return rcopy(ref, ref, c_ss.at[k, h, 1], c_rs.at[k, h, 1], (((y + i) % NY) * 2 + core, me))
 
     def half_copy(k, h):
         arr = C2 if k == 0 else out_ref
@@ -475,8 +474,9 @@
             row_copy(k, h, i).start()
 
     def rows_pass(k, h):
-        for i in (1, 3, 2):
-            row_copy(k, h, i).wait_recv()
+        arr = C2 if k == 0 else out_ref
+        got = arr.at[pl.ds(0, 3 * RQ)]
+        rcopy(got, got, c_ss.at[k, h, 1], c_rs.at[k, h, 1], sib).wait_recv()
         half_copy(k, h).start()
 
     def rows_wait(k, h):
@@ -485,21 +485,15 @@
     def reduce_drain(it):
         for h in range(CH):
             pair_copy(it, h).wait_send()
-            for i in range(1, NY):
-                y_copy(it, h, i).wait_send()
-                row_copy(it, h, i).wait_send()
+            sent = rb2n.at[it, h, pl.ds(1, NY - 1)]
+            rcopy(sent, sent, n2_ss.at[it, h], n2_rs.at[it, h], sib).wait_send()
+            arr = C2 if it == 0 else out_ref
+            sent = arr.at[pl.ds(0, 3 * RQ)]
+            rcopy(sent, sent, c_ss.at[it, h, 1], c_rs.at[it, h, 1], sib).wait_send()
             half_copy(it, h).wait_send()
 
-    def finish():
-        if STOP < 1:
-            early_drain()
-        if STOP < 90:
-            out_ref[...] = jnp.zeros_like(out_ref)
-            loss_ref[...] = jnp.zeros_like(loss_ref)
-
     def early_drain():
-        if STOP >= 0:
-            gather_drain()
+        gather_drain()
 
         def wsq(o, _):
             q_copy(o, dp).wait_send()
@@ -524,36 +518,10 @@
         for h in range(CH):
             pair_sum(it, h)
 
-    if STOP == -2:
-        for o in range(1, DP):
-            q_copy(o, dp).start()
-        lax.fori_loop(1, DP, q_wait, 0)
-        for i in range(2, 5):
-            loads[i].wait()
-        return finish()
-    if STOP == -1:
-        for o in range(1, DP):
-            q_copy(o, dp).start()
-        early()
-        return finish()
-    if STOP == 0:
-        gather(lambda d: None)
-        return finish()
     softmax_first()
     owner_combine(0)
     early_drain()
-    if STOP == 1:
-        stats_wait(0, NEAR)
-        stats_wait(0, FAR)
-        stats_drain(0)
-        return finish()
     query_post()
-    if STOP == 2:
-        stats_wait(0, NEAR)
-        stats_wait(0, FAR)
-        stats_drain(0)
-        query_finish()
-        return finish()
     mid(0)
     for h in range(CH):
         newc = update(0, h)
@@ -564,22 +532,10 @@
     stats_drain(0)
     for h in range(CH):
         rows_pass(0, h)
-    if STOP == 5:
-        for h in range(CH):
-            rows_wait(0, h)
-        reduce_drain(0)
-        query_finish()
-        return finish()
 
     softmax_second()
     owner_combine(1)
     query_finish()
-    if STOP == 6:
-        stats_wait(1, NEAR)
-        stats_wait(1, FAR)
-        stats_drain(1)
-        reduce_drain(0)
-        return finish()
     mid(1)
     for h in range(CH):
         out_ref[quarter(h, y), :] = update(1, h).astype(BF16)
@@ -591,7 +547,6 @@
     for h in range(CH):
         rows_wait(1, h)
     reduce_drain(1)
-    finish()
 
 
 def on_device(passages, queries, init_centroids, pattern, positive_offset):
@@ -614,7 +569,6 @@
             pltpu.VMEM((2, CH, RH, W), F32),
             pltpu.VMEM((2, CH, RH, W), BF16),
             pltpu.VMEM((2, CH, NY, RQ, W), BF16),
-            pltpu.VMEM((2, CH, NY, RQ, W), F32),
             pltpu.VMEM((CH, RQ, D), F32),
             pltpu.VMEM((KL, D), F32),
             pltpu.VMEM((4, D), BF16),
@@ -634,8 +588,8 @@
             dma((2,)), dma((2,)),
             dma((2,)), dma((2, 2)),
             dma((2, CH)), dma((2, CH)),
-            dma((2, CH, NY)), dma((2, CH, NY)),
-            dma((2, CH, NY)), dma((2, CH, NY)),
+            dma((2, CH)), dma((2, CH)),
+            dma((2, CH, 2)), dma((2, CH, 2)),
             dma((DP,)), dma((DP,)),
             dma((5,)),
         ],

time: 100 us -> 99.8 us (level)
  no operation moved by 1% of the time
where the time goes in v7:
time: 99.8 us; the launch traced here: 99.7 us
  Pallas kernels  96.6 us (97%)
  other arithmetic  1.93 us (2%)
    pallas_call x1, Pallas kernels, on_device(): pl.pallas_call(kernel, out_shape=(jax.ShapeDtypeStruct((KL, D), BF16), ja...  96.6 us

profile of v7, /device:TPU:1, one launch (start us, length us, event | category | flops | bytes accessed | tf_op | source)
XLA Modules:
  0.0 99.7 jit_solution(12242868452071917118)
XLA Ops:
  0.6 96.6 %shard_map.68 = (bf16[256,768]{1,0:T(8,128)(2,1)}, f32[1,4]{1,0:T(1,128)}) custom-call(bf16[128,768]{1,0:T(8,128)(2,1)} %p_ref.1, bf16[4,768]{1,0:T(4,128)(2,1)} %q_ref.1, f32[256,768]{1,0:T(8,128)} %c_ref.1, s32[4,1024]{1,0:T(4,128)} %bitcast.3, s32[8,128]{1,0:T(8,128)} %bitcast.4), custom_call_target="tpu_custom_call" | custom-call | tf_op jit(solution)/shard_map/pallas_call | solution.py:556
  97.2 0.0 copy-start
  97.2 1.9 %convert_element_type.3 = f32[256,768]{1,0:T(8,128)} convert(bf16[256,768]{1,0:T(8,128)(2,1)} %get-tuple-element.4) | non-fusion elementwise | flops 196608 | bytes 1179648 | tf_op jit(solution)/shard_map/convert_element_type | solution.py:600
  99.2 0.0 copy-done
  99.2 0.5 copy.8
Async XLA Ops:
  97.2 1.9 %copy-start = (f32[1,4]{1,0:T(1,128)S(1)}, f32[1,4]{1,0:T(1,128)}, u32[]{:S(2)}) copy-start(f32[1,4]{1,0:T(1,128)} %get-tuple-element.5) | copy-start | bytes 52

commit v8 on v7

--- a/solution.py
+++ b/solution.py
@@ -260,11 +260,11 @@
     def ship(it, zc, mine):
         if mine:
             st_r[it, z * NX + x] = st_s[z4 * NX + x]
-            for i in range(1, NX):
+            for i in (2, 1, 3):
                 st_copy(it, (x + i) % NX, z4, x, z).start()
         else:
-            for xc in range(NX):
-                st_copy(it, xc, zc, x, z).start()
+            for i in (2, 1, 3, 0):
+                st_copy(it, (x + i) % NX, zc, x, z).start()
 
     def columns(it, zcs):
         for zc in zcs:
@@ -520,7 +520,6 @@
 
     softmax_first()
     owner_combine(0)
-    early_drain()
     query_post()
     mid(0)
     for h in range(CH):
@@ -529,6 +528,7 @@
         C2[quarter(h, y), 0:D] = newc.astype(BF16)
         C2[quarter(h, y), D:W] = three(jnp.sum(newc * newc, axis=1, keepdims=True), RQ)
         rows_send(0, h)
+    early_drain()
     stats_drain(0)
     for h in range(CH):
         rows_pass(0, h)

time: 99.8 us -> 99.7 us (level)
  no operation moved by 1% of the time
where the time goes in v8:
time: 99.7 us; the launch traced here: 99.6 us
  Pallas kernels  96.5 us (97%)
  other arithmetic  1.93 us (2%)
    pallas_call x1, Pallas kernels, on_device(): pl.pallas_call(kernel, out_shape=(jax.ShapeDtypeStruct((KL, D), BF16), ja...  96.5 us

profile of v8, /device:TPU:1, one launch (start us, length us, event | category | flops | bytes accessed | tf_op | source)
XLA Modules:
  0.0 99.6 jit_solution(4312390667483616506)
XLA Ops:
  0.6 96.5 %shard_map.68 = (bf16[256,768]{1,0:T(8,128)(2,1)}, f32[1,4]{1,0:T(1,128)}) custom-call(bf16[128,768]{1,0:T(8,128)(2,1)} %p_ref.1, bf16[4,768]{1,0:T(4,128)(2,1)} %q_ref.1, f32[256,768]{1,0:T(8,128)} %c_ref.1, s32[4,1024]{1,0:T(4,128)} %bitcast.3, s32[8,128]{1,0:T(8,128)} %bitcast.4), custom_call_target="tpu_custom_call" | custom-call | tf_op jit(solution)/shard_map/pallas_call | solution.py:556
  97.2 0.0 copy-start
  97.2 1.9 %convert_element_type.3 = f32[256,768]{1,0:T(8,128)} convert(bf16[256,768]{1,0:T(8,128)(2,1)} %get-tuple-element.4) | non-fusion elementwise | flops 196608 | bytes 1179648 | tf_op jit(solution)/shard_map/convert_element_type | solution.py:600
  99.1 0.0 copy-done
  99.1 0.5 copy.8
Async XLA Ops:
  97.2 1.9 %copy-start = (f32[1,4]{1,0:T(1,128)S(1)}, f32[1,4]{1,0:T(1,128)}, u32[]{:S(2)}) copy-start(f32[1,4]{1,0:T(1,128)} %get-tuple-element.5) | copy-start | bytes 52
